TPU v7x, 128 devices: a whole 4x4x4 slice. The times are simulated.
128 devices in a mesh: dp: 16 (over z_lo, x, core), tensor: 8 (over y, z_hi).
Axes of the slice: x: 4, y: 4, z: 4 (z_hi: 2, z_lo: 2; z = z_hi * 2 + z_lo), core: 2. Of those that a mesh axis runs over, the one named last changes fastest.
Arguments:
- block_in: float32 [16384, 1024], P(('dp', 'tensor')), may hold values from -45 to 45
- norm1_gain: float32 [1024], replicated, may hold values from 0.25 to 1.75
- w_b: bfloat16 [1024, 1024], P('dp', 'tensor'), may hold values from -0.1875 to 0.1875
- w_c: bfloat16 [1024, 1024], P('dp', 'tensor'), may hold values from -0.1875 to 0.1875
- w_x: bfloat16 [1024, 1024], P('dp', 'tensor'), may hold values from -0.1875 to 0.1875
- conv_w: float32 [3, 1024], P(None, 'tensor'), may hold values from -3.5 to 3.5
- w_out: bfloat16 [1024, 1024], P('tensor', 'dp'), may hold values from -0.1875 to 0.1875
- norm2_gain: float32 [1024], replicated, may hold values from 0.25 to 1.75
- w_gate: bfloat16 [1024, 4608], P('dp', 'tensor'), may hold values from -0.1875 to 0.1875
- w_up: bfloat16 [1024, 4608], P('dp', 'tensor'), may hold values from -0.1875 to 0.1875
- w_down: bfloat16 [4608, 1024], P('tensor', 'dp'), may hold values from -0.09375 to 0.09375
- out_cot: float32 [16384, 1024], P(('dp', 'tensor')), may hold values from -6 to 6
Outputs:
- block_out: float32 [16384, 1024], P(('dp', 'tensor'))
- grad_in: float32 [16384, 1024], P(('dp', 'tensor'))
- grad_norm1: float32 [1024], replicated
- grad_w_b: float32 [1024, 1024], P('dp', 'tensor')
- grad_w_c: float32 [1024, 1024], P('dp', 'tensor')
- grad_w_x: float32 [1024, 1024], P('dp', 'tensor')
- grad_conv: float32 [3, 1024], P(None, 'tensor')
- grad_w_out: float32 [1024, 1024], P('tensor', 'dp')
- grad_norm2: float32 [1024], replicated
- grad_w_gate: float32 [1024, 4608], P('dp', 'tensor')
- grad_w_up: float32 [1024, 4608], P('dp', 'tensor')
- grad_w_down: float32 [4608, 1024], P('tensor', 'dp')
All inputs are finite; a program needn't handle non-finite values.
Results may differ from a plain program's by a relative error of at most 0.022.
Values may be sent and summed in bfloat16 or wider, within the bound.
A program may use at most 64 MiB of HBM per device.

v0:
```python
import jax
import jax.numpy as jnp
from jax import lax
from jax.sharding import PartitionSpec as P

SEQ = 2048
OFFSET = 512


EPS = 1e-06


def passed_along(block, axis, distance):
    devices = range(lax.axis_size(axis))
    route = [(i - distance, i) for i in devices if i - distance in devices]
    return lax.ppermute(block, axis, route)


def tdot(left, right):
    return lax.dot_general(
        left, right, (((0,), (0,)), ((), ())), preferred_element_type=jnp.float32
    )


def ndot(left, right):
    return lax.dot_general(
        left, right, (((1,), (1,)), ((), ())), preferred_element_type=jnp.float32
    )


def seq_gather(values):
    return lax.all_gather(values.astype(jnp.bfloat16), "tensor", axis=0, tiled=True)


def seq_scatter(values):
    return lax.psum_scatter(
        values.astype(jnp.bfloat16), "tensor", scatter_dimension=0, tiled=True
    ).astype(jnp.float32)


def seq_masks(rows):
    segment = (rows + SEQ - OFFSET) // SEQ
    mask_one = jnp.where((rows >= 1) & ((rows - 1 + SEQ - OFFSET) // SEQ == segment), 1.0, 0.0)
    mask_two = jnp.where((rows >= 2) & ((rows - 2 + SEQ - OFFSET) // SEQ == segment), 1.0, 0.0)
    return (mask_one.astype(jnp.float32), mask_two.astype(jnp.float32))


def per_device(
    block_in, norm1_gain, w_b, w_c, w_x, conv_w, w_out, norm2_gain, w_gate, w_up, w_down, out_cot
):
    length = block_in.shape[0] * lax.axis_size("tensor")
    dp_index = lax.axis_index("dp")
    fetched = (
        lax.all_gather(w_b, "dp", axis=0, tiled=True),
        lax.all_gather(w_c, "dp", axis=0, tiled=True),
        lax.all_gather(w_x, "dp", axis=0, tiled=True),
        lax.all_gather(w_out, "dp", axis=1, tiled=True),
        lax.all_gather(w_gate, "dp", axis=0, tiled=True),
        lax.all_gather(w_up, "dp", axis=0, tiled=True),
        lax.all_gather(w_down, "dp", axis=1, tiled=True),
    )
    full_b, full_c, full_x, full_out, full_gate, full_up, full_down = fetched
    positions = dp_index * length + jnp.arange(length, dtype=jnp.int32)[:, None]
    mask_one, mask_two = seq_masks(positions)
    r1 = lax.rsqrt(jnp.mean(block_in * block_in, -1, keepdims=True) + EPS)
    n1 = block_in * r1
    h1 = seq_gather(n1 * norm1_gain)
    bproj = jnp.dot(h1, full_b, preferred_element_type=jnp.float32)
    cproj = jnp.dot(h1, full_c, preferred_element_type=jnp.float32)
    xproj = jnp.dot(h1, full_x, preferred_element_type=jnp.float32)
    gated = bproj * xproj
    incoming = passed_along(gated[-2:], "dp", 1)
    extended = jnp.concatenate([incoming, gated], 0)
    conv = (
        conv_w[0] * extended[:-2] * mask_two
        + conv_w[1] * extended[1:-1] * mask_one
        + conv_w[2] * gated
    )
    ymix = (cproj * conv).astype(jnp.bfloat16)
    mid = block_in + seq_scatter(jnp.dot(ymix, full_out, preferred_element_type=jnp.float32))
    r2 = lax.rsqrt(jnp.mean(mid * mid, -1, keepdims=True) + EPS)
    n2 = mid * r2
    h2 = seq_gather(n2 * norm2_gain)
    gate = jnp.dot(h2, full_gate, preferred_element_type=jnp.float32)
    up = jnp.dot(h2, full_up, preferred_element_type=jnp.float32)
    sig = jax.nn.sigmoid(gate)
    act = (gate * sig * up).astype(jnp.bfloat16)
    block_out = mid + seq_scatter(jnp.dot(act, full_down, preferred_element_type=jnp.float32))
    refetched = (
        lax.all_gather(w_b, "dp", axis=0, tiled=True),
        lax.all_gather(w_c, "dp", axis=0, tiled=True),
        lax.all_gather(w_x, "dp", axis=0, tiled=True),
        lax.all_gather(w_out, "dp", axis=1, tiled=True),
        lax.all_gather(w_gate, "dp", axis=0, tiled=True),
        lax.all_gather(w_up, "dp", axis=0, tiled=True),
        lax.all_gather(w_down, "dp", axis=1, tiled=True),
    )
    full_b, full_c, full_x, full_out, full_gate, full_up, full_down = refetched
    cot_full = seq_gather(out_cot)
    g_down = tdot(act, cot_full)
    dact = ndot(cot_full, full_down)
    dgate = (dact * up * sig * (1.0 + gate * (1.0 - sig))).astype(jnp.bfloat16)
    dup = (dact * gate * sig).astype(jnp.bfloat16)
    g_gate = tdot(h2, dgate)
    g_up = tdot(h2, dup)
    dh2 = seq_scatter(ndot(dgate, full_gate) + ndot(dup, full_up))
    part_n2 = jnp.sum(dh2 * n2, 0)
    dn2 = dh2 * norm2_gain
    dmid = out_cot + r2 * (dn2 - n2 * jnp.mean(dn2 * n2, -1, keepdims=True))
    dmid_full = seq_gather(dmid)
    g_out = tdot(ymix, dmid_full)
    dy = ndot(dmid_full, full_out)
    dc = (dy * conv).astype(jnp.bfloat16)
    dconv = dy * cproj
    masked_one = dconv * mask_one
    masked_two = dconv * mask_two
    outgoing = passed_along(jnp.concatenate([masked_one[:1], masked_two[:2]], 0), "dp", -1)
    next_one = jnp.concatenate([masked_one[1:], outgoing[:1]], 0)
    next_two = jnp.concatenate([masked_two[2:], outgoing[1:]], 0)
    dgated = conv_w[2] * dconv + conv_w[1] * next_one + conv_w[0] * next_two
    part_conv = jnp.stack(
        [
            jnp.sum(dconv * extended[:-2] * mask_two, 0),
            jnp.sum(dconv * extended[1:-1] * mask_one, 0),
            jnp.sum(dconv * gated, 0),
        ],
        0,
    )
    db = (dgated * xproj).astype(jnp.bfloat16)
    dx = (dgated * bproj).astype(jnp.bfloat16)
    g_b = tdot(h1, db)
    g_c = tdot(h1, dc)
    g_x = tdot(h1, dx)
    dh1 = seq_scatter(ndot(db, full_b) + ndot(dc, full_c) + ndot(dx, full_x))
    part_n1 = jnp.sum(dh1 * n1, 0)
    dn1 = dh1 * norm1_gain
    grad_in = dmid + r1 * (dn1 - n1 * jnp.mean(dn1 * n1, -1, keepdims=True))
    owned = (
        lax.psum_scatter(g_b.astype(jnp.bfloat16), "dp", scatter_dimension=0, tiled=True).astype(
            jnp.float32
        ),
        lax.psum_scatter(g_c.astype(jnp.bfloat16), "dp", scatter_dimension=0, tiled=True).astype(
            jnp.float32
        ),
        lax.psum_scatter(g_x.astype(jnp.bfloat16), "dp", scatter_dimension=0, tiled=True).astype(
            jnp.float32
        ),
        lax.psum_scatter(g_out.astype(jnp.bfloat16), "dp", scatter_dimension=1, tiled=True).astype(
            jnp.float32
        ),
        lax.psum_scatter(g_gate.astype(jnp.bfloat16), "dp", scatter_dimension=0, tiled=True).astype(
            jnp.float32
        ),
        lax.psum_scatter(g_up.astype(jnp.bfloat16), "dp", scatter_dimension=0, tiled=True).astype(
            jnp.float32
        ),
        lax.psum_scatter(g_down.astype(jnp.bfloat16), "dp", scatter_dimension=1, tiled=True).astype(
            jnp.float32
        ),
    )
    channels = conv_w.shape[1]
    offset = lax.axis_index("tensor") * channels
    placed = lax.dynamic_update_slice(
        jnp.zeros((3, channels * lax.axis_size("tensor")), jnp.float32),
        part_conv,
        (jnp.int32(0), offset),
    )
    sum_n1, sum_n2, sum_conv = lax.psum((part_n1, part_n2, placed), ("dp", "tensor"))
    grad_conv = lax.dynamic_slice(sum_conv, (jnp.int32(0), offset), (3, channels))
    return (
        block_out,
        grad_in,
        sum_n1,
        owned[0],
        owned[1],
        owned[2],
        grad_conv,
        owned[3],
        sum_n2,
        owned[4],
        owned[5],
        owned[6],
    )


def solution(mesh):
    placed = (
        P(("dp", "tensor"), None),
        P(),
        P("dp", "tensor"),
        P("dp", "tensor"),
        P("dp", "tensor"),
        P(None, "tensor"),
        P("tensor", "dp"),
        P(),
        P("dp", "tensor"),
        P("dp", "tensor"),
        P("tensor", "dp"),
        P(("dp", "tensor"), None),
    )
    return jax.shard_map(
        per_device,
        mesh=mesh,
        in_specs=placed,
        out_specs=(
            P(("dp", "tensor"), None),
            P(("dp", "tensor"), None),
            P(),
            P("dp", "tensor"),
            P("dp", "tensor"),
            P("dp", "tensor"),
            P(None, "tensor"),
            P("tensor", "dp"),
            P(),
            P("dp", "tensor"),
            P("dp", "tensor"),
            P("tensor", "dp"),
        ),
        check_vma=False,
    )
```

profile of v0, /device:TPU:0, one launch (start us, length us, event | category | flops | bytes accessed | tf_op | source)
XLA Modules:
  0.0 1058.4 jit_solution(17227127163043565539)
XLA Ops:
  8.1 1.2 multiply_reduce_fusion.4
  9.3 1.9 multiply_convert_fusion.8
  11.2 21.1 %all_gather.42 = bf16[1024,128]{1,0:T(8,128)(2,1)S(1)} all-gather(bf16[64,128]{1,0:T(8,128)(2,1)} %param.14), channel_id=1, replica_groups=mesh['dp'=16,'tensor'=8] {'dp'}, dimensions={0}, use_global_device_ids=true | all-gather | bytes 278528 | tf_op jit(solution)/shard_map/all_gather | solution.py:54
  32.3 18.7 %all_gather.41 = bf16[1024,128]{1,0:T(8,128)(2,1)} all-gather(bf16[64,128]{1,0:T(8,128)(2,1)} %param.15), channel_id=1, replica_groups=mesh['dp'=16,'tensor'=8] {'dp'}, dimensions={0}, use_global_device_ids=true | all-gather | bytes 278528 | tf_op jit(solution)/shard_map/all_gather | solution.py:55
  51.0 18.2 %all_gather.43 = bf16[1024,128]{1,0:T(8,128)(2,1)S(1)} all-gather(bf16[64,128]{1,0:T(8,128)(2,1)S(1)} %copy-done.27), channel_id=1, replica_groups=mesh['dp'=16,'tensor'=8] {'dp'}, dimensions={0}, use_global_device_ids=true | all-gather | bytes 278528 | tf_op jit(solution)/shard_map/all_gather | solution.py:56
  69.2 17.1 %all_gather.44 = bf16[128,1024]{0,1:T(8,128)(2,1)S(1)} all-gather(bf16[128,64]{0,1:T(8,128)(2,1)S(1)} %copy-done.28), channel_id=1, replica_groups=mesh['dp'=16,'tensor'=8] {'dp'}, dimensions={1}, use_global_device_ids=true | all-gather | bytes 278528 | tf_op jit(solution)/shard_map/all_gather | solution.py:57
  86.3 2.4 fusion.38
  88.8 1.5 fusion.37
  90.3 2.3 collective-permute-start
  92.6 0.8 collective-permute-done
  93.4 1.7 multiply_convert_fusion.7
  95.1 2.1 convolution_convert_fusion.1
  97.9 79.0 %reduce-scatter.12.cloned.1.call-done = bf16[128,1024]{1,0:T(8,128)(2,1)} async-done(((bf16[1024,1024]{1,0:T(8,128)(2,1)}), bf16[128,1024]{1,0:T(8,128)(2,1)}) %reduce-scatter.12.cloned.1.call-update) | async-done | bytes 262160 | tf_op jit(solution)/shard_map/reduce_scatter | solution.py:36
  176.9 1.1 multiply_reduce_fusion.3
  178.0 1.8 multiply_convert_fusion.6
  182.2 51.3 %all-gather.10.cloned.1.call-done = bf16[1024,1024]{1,0:T(8,128)(2,1)} async-done(((bf16[128,1024]{1,0:T(8,128)(2,1)}), bf16[1024,1024]{1,0:T(8,128)(2,1)}) %all-gather.10.cloned.1.call-update) | async-done | bytes 2097168 | tf_op jit(solution)/shard_map/all_gather | solution.py:32
  233.5 4.8 fusion.40
  238.3 28.0 %all-gather.12.cloned.1.call-done = bf16[1024,576]{1,0:T(8,128)(2,1)} async-done(((bf16[64,576]{1,0:T(8,128)(2,1)}), bf16[1024,576]{1,0:T(8,128)(2,1)}) %all-gather.12.cloned.1.call-update) | async-done | bytes 1179664 | tf_op jit(solution)/shard_map/all_gather | solution.py:58
  266.3 4.8 fusion.39
  271.1 29.6 %all-gather.16.cloned.1.call-done = bf16[576,1024]{0,1:T(8,128)(2,1)} async-done(((bf16[576,64]{0,1:T(8,128)(2,1)}), bf16[576,1024]{0,1:T(8,128)(2,1)}) %all-gather.16.cloned.1.call-update) | async-done | bytes 1179664 | tf_op jit(solution)/shard_map/all_gather | solution.py:60
  300.7 57.6 %all-gather.18.cloned.1.call-done = bf16[1024,1024]{1,0:T(8,128)(2,1)} async-done(((bf16[128,1024]{1,0:T(8,128)(2,1)}), bf16[1024,1024]{1,0:T(8,128)(2,1)}) %all-gather.18.cloned.1.call-update) | async-done | bytes 2097168 | tf_op jit(solution)/shard_map/all_gather | solution.py:32
  358.3 6.9 multiply_convert_fusion
  365.2 1.8 fusion.41
  367.4 3.2 add_convert_fusion.1
  370.7 75.4 %reduce-scatter.16.cloned.1.call-done = bf16[128,1024]{1,0:T(8,128)(2,1)} async-done(((bf16[1024,1024]{1,0:T(8,128)(2,1)}), bf16[128,1024]{1,0:T(8,128)(2,1)}) %reduce-scatter.16.cloned.1.call-update) | async-done | bytes 262160 | tf_op jit(solution)/shard_map/reduce_scatter | solution.py:36
  446.0 1.2 fusion.11
  447.3 1.9 fusion.35
  449.2 4.9 convolution_convert_fusion.2
  454.4 4.9 convolution_convert_fusion.3
  459.4 4.9 convolution_convert_fusion.4
  464.4 40.4 %all-gather.20.cloned.1.call-done = bf16[1024,1024]{1,0:T(8,128)(2,1)} async-done(((bf16[128,1024]{1,0:T(8,128)(2,1)}), bf16[1024,1024]{1,0:T(8,128)(2,1)}) %all-gather.20.cloned.1.call-update) | async-done | bytes 2097168 | tf_op jit(solution)/shard_map/all_gather | solution.py:32
  504.8 3.3 convolution_convert_fusion.5
  508.2 2.4 fusion.42
  511.1 0.9 copy-done.7
  513.3 1.3 collective-permute-start.1
  514.6 1.5 convolution_convert_fusion.7
  516.0 1.9 slice.56
  517.9 1.9 slice.59
  519.9 2.4 multiply_convert_fusion.3
  523.1 1.5 convolution_convert_fusion.8
  524.6 3.8 fusion.44
  528.4 1.5 convolution_convert_fusion.6
  530.0 1.9 fusion.43
  532.5 2.1 add_convert_fusion
  535.0 1.0 copy-done.30
  535.9 4.5 convolution_convert_fusion
  540.5 1.6 convert_element_type.131
  542.1 37.7 %reduce-scatter.30.cloned.1.call-done = bf16[64,576]{1,0:T(8,128)(2,1)} async-done(((bf16[1024,576]{1,0:T(8,128)(2,1)}), bf16[64,576]{1,0:T(8,128)(2,1)}) %reduce-scatter.30.cloned.1.call-update) | async-done | bytes 73744 | tf_op jit(solution)/shard_map/reduce_scatter | solution.py:154
  579.7 1.6 convert_element_type.129
  581.3 62.0 %reduce-scatter.28.cloned.1.call-done = bf16[64,576]{1,0:T(8,128)(2,1)} async-done(((bf16[1024,576]{1,0:T(8,128)(2,1)}), bf16[64,576]{1,0:T(8,128)(2,1)}) %reduce-scatter.28.cloned.1.call-update) | async-done | bytes 73744 | tf_op jit(solution)/shard_map/reduce_scatter | solution.py:151
  643.3 1.6 convert_element_type.127
  644.9 60.3 %reduce-scatter.26.cloned.1.call-done = bf16[128,64]{0,1:T(8,128)(2,1)} async-done(((bf16[128,1024]{0,1:T(8,128)(2,1)}), bf16[128,64]{0,1:T(8,128)(2,1)}) %reduce-scatter.26.cloned.1.call-update) | async-done | bytes 16400 | tf_op jit(solution)/shard_map/reduce_scatter | solution.py:148
  705.1 1.3 convert_element_type.125
  706.4 60.7 %reduce-scatter.22.cloned.1.call-done = bf16[64,128]{1,0:T(8,128)(2,1)} async-done(((bf16[1024,128]{1,0:T(8,128)(2,1)}), bf16[64,128]{1,0:T(8,128)(2,1)}) %reduce-scatter.22.cloned.1.call-update) | async-done | bytes 16400 | tf_op jit(solution)/shard_map/reduce_scatter | solution.py:142
  767.1 1.3 convert_element_type.121
  768.4 60.4 %reduce-scatter.20.cloned.1.call-done = bf16[64,128]{1,0:T(8,128)(2,1)} async-done(((bf16[1024,128]{1,0:T(8,128)(2,1)}), bf16[64,128]{1,0:T(8,128)(2,1)}) %reduce-scatter.20.cloned.1.call-update) | async-done | bytes 16400 | tf_op jit(solution)/shard_map/reduce_scatter | solution.py:139
  828.8 1.3 convert_element_type.119
  830.2 60.5 %reduce-scatter.24.cloned.1.call-done = bf16[64,128]{1,0:T(8,128)(2,1)} async-done(((bf16[1024,128]{1,0:T(8,128)(2,1)}), bf16[64,128]{1,0:T(8,128)(2,1)}) %reduce-scatter.24.cloned.1.call-update) | async-done | bytes 16400 | tf_op jit(solution)/shard_map/reduce_scatter | solution.py:145
  890.7 1.3 convert_element_type.123
  892.0 77.4 %reduce-scatter.18.cloned.1.call-done = bf16[128,1024]{1,0:T(8,128)(2,1)} async-done(((bf16[1024,1024]{1,0:T(8,128)(2,1)}), bf16[128,1024]{1,0:T(8,128)(2,1)}) %reduce-scatter.18.cloned.1.call-update) | async-done | bytes 262160 | tf_op jit(solution)/shard_map/reduce_scatter | solution.py:36
  969.5 1.2 fusion.12
  970.7 66.0 %all-reduce = (f32[1024]{0:T(1024)}, f32[3,1024]{1,0:T(4,128)S(1)}, f32[1024]{0:T(1024)}) all-reduce(f32[1024]{0:T(1024)S(1)} %get-tuple-element.17, f32[3,1024]{1,0:T(4,128)S(1)} %maximum_dynamic-update-slice_fusion, f32[1024]{0:T(1024)S(1)} %get-tuple-element.14), channel_id=1, replica_groups=mesh['dp'=16,'tensor'=8] {'dp','tensor'}, use_global_device_ids=true, to_apply=%region_9.10 | all-reduce | flops 5120 | bytes 40960 | tf_op jit(solution)/shard_map/psum | solution.py:168
  1037.3 11.5 %reduce-scatter.14.cloned.1.call-done = bf16[128,1024]{1,0:T(8,128)(2,1)} async-done(((bf16[1024,1024]{1,0:T(8,128)(2,1)}), bf16[128,1024]{1,0:T(8,128)(2,1)}) %reduce-scatter.14.cloned.1.call-update) | async-done | bytes 262160 | tf_op jit(solution)/shard_map/reduce_scatter | solution.py:36
  1048.8 2.3 fusion.7
  (127 shorter events, 8.3 us)
Async XLA Ops:
  8.0 43.0 %copy-start.27 = (bf16[64,128]{1,0:T(8,128)(2,1)S(1)}, bf16[64,128]{1,0:T(8,128)(2,1)}, u32[]{:S(2)}) copy-start(bf16[64,128]{1,0:T(8,128)(2,1)} %param.16) | copy-start | bytes 49156
  8.0 61.1 %copy-start.28 = (bf16[128,64]{0,1:T(8,128)(2,1)S(1)}, bf16[128,64]{0,1:T(8,128)(2,1)}, u32[]{:S(2)}) copy-start(bf16[128,64]{0,1:T(8,128)(2,1)} %param.18) | copy-start | bytes 49156
  8.0 78.2 %copy-start.29 = (f32[3,128]{1,0:T(4,128)S(1)}, f32[3,128]{1,0:T(4,128)}, u32[]{:S(2)}) copy-start(f32[3,128]{1,0:T(4,128)} %param.17) | copy-start | bytes 4612
  8.0 78.2 %all-gather.8.cloned.1.call-start = ((), (), s32[]{:S(2)}) async-start(), calls=%async_computation.11 | async-start | bytes 2359296 | tf_op jit(solution)/shard_map/all_gather | solution.py:32
  11.2 165.7 %reduce-scatter.12.cloned.1.call-start = ((), (), s32[]{:S(2)}) async-start(), calls=%async_computation.12 | async-start | bytes 2359296 | tf_op jit(solution)/shard_map/reduce_scatter | solution.py:36
  32.3 58.0 %copy-start.16 = (bf16[1024,128]{1,0:T(8,128)(2,1)}, bf16[1024,128]{1,0:T(8,128)(2,1)S(1)}, u32[]{:S(2)}) copy-start(bf16[1024,128]{1,0:T(8,128)(2,1)S(1)} %all_gather.42) | copy-start | bytes 786436
  69.2 21.1 %copy-start.13 = (bf16[1024,128]{1,0:T(8,128)(2,1)}, bf16[1024,128]{1,0:T(8,128)(2,1)S(1)}, u32[]{:S(2)}) copy-start(bf16[1024,128]{1,0:T(8,128)(2,1)S(1)} %all_gather.43) | copy-start | bytes 786436
  86.3 8.9 copy-start.15
  86.3 2.5 copy-start
  88.8 6.4 copy-start.5
  88.8 4.6 copy-start.22
  90.3 4.8 copy-start.18
  90.3 3.1 collective-permute-start
  95.1 2.1 copy-start.21
  95.1 81.7 %copy-start.1 = (f32[128,1024]{1,0:T(8,128)S(1)}, f32[128,1024]{1,0:T(8,128)}, u32[]{:S(2)}) copy-start(f32[128,1024]{1,0:T(8,128)} %param.12) | copy-start | bytes 1572868
  97.2 80.8 %copy-start.25 = (f32[1024]{0:T(1024)S(1)}, f32[1024]{0:T(1024)}, u32[]{:S(2)}) copy-start(f32[1024]{0:T(1024)} %param.19) | copy-start | bytes 12292
  97.2 83.9 %copy-start.4 = (f32[128,1024]{1,0:T(8,128)S(1)}, f32[128,1024]{1,0:T(8,128)}, u32[]{:S(2)}) copy-start(f32[128,1024]{1,0:T(8,128)} %param.23) | copy-start | bytes 1572868
  97.2 84.9 %all-gather.14.cloned.1.call-start = ((), (), s32[]{:S(2)}) async-start(), calls=%async_computation.15 | async-start | bytes 1392640 | tf_op jit(solution)/shard_map/all_gather | solution.py:59
  97.8 135.7 %all-gather.10.cloned.1.call-start = ((), (), s32[]{:S(2)}) async-start(), calls=%async_computation.13 | async-start | bytes 2359296 | tf_op jit(solution)/shard_map/all_gather | solution.py:32
  179.8 86.5 %all-gather.12.cloned.1.call-start = ((), (), s32[]{:S(2)}) async-start(), calls=%async_computation.14 | async-start | bytes 1392640 | tf_op jit(solution)/shard_map/all_gather | solution.py:58
  180.4 120.4 %all-gather.16.cloned.1.call-start = ((), (), s32[]{:S(2)}) async-start(), calls=%async_computation.16 | async-start | bytes 1392640 | tf_op jit(solution)/shard_map/all_gather | solution.py:60
  181.1 177.2 %all-gather.18.cloned.1.call-start = ((), (), s32[]{:S(2)}) async-start(), calls=%async_computation.18 | async-start | bytes 2359296 | tf_op jit(solution)/shard_map/all_gather | solution.py:32
  181.9 264.1 %reduce-scatter.16.cloned.1.call-start = ((), (), s32[]{:S(2)}) async-start(), calls=%async_computation.19 | async-start | bytes 2359296 | tf_op jit(solution)/shard_map/reduce_scatter | solution.py:36
  358.3 6.9 copy-start.32
  365.2 1.9 copy-start.34
  365.2 1.9 copy-start.33
  365.2 2.2 copy-start.31
  370.6 75.4 %copy-start.3 = (bf16[128,1024]{1,0:T(8,128)(2,1)S(1)}, bf16[128,1024]{1,0:T(8,128)(2,1)}, u32[]{:S(2)}) copy-start(bf16[128,1024]{1,0:T(8,128)(2,1)} %reduce-scatter.12.cloned.1.call-done) | copy-start | bytes 786436
  370.6 134.2 %all-gather.20.cloned.1.call-start = ((), (), s32[]{:S(2)}) async-start(), calls=%async_computation.20 | async-start | bytes 2359296 | tf_op jit(solution)/shard_map/all_gather | solution.py:32
  449.2 91.3 %reduce-scatter.32.cloned.1.call-start = ((), (), s32[]{:S(2)}) async-start(), calls=%async_computation.28 | async-start | bytes 1392640 | tf_op jit(solution)/shard_map/reduce_scatter | solution.py:157
  454.2 125.6 %reduce-scatter.30.cloned.1.call-start = ((), (), s32[]{:S(2)}) async-start(), calls=%async_computation.27 | async-start | bytes 1392640 | tf_op jit(solution)/shard_map/reduce_scatter | solution.py:154
  459.3 183.9 %reduce-scatter.28.cloned.1.call-start = ((), (), s32[]{:S(2)}) async-start(), calls=%async_computation.26 | async-start | bytes 1392640 | tf_op jit(solution)/shard_map/reduce_scatter | solution.py:151
  464.3 240.8 %reduce-scatter.26.cloned.1.call-start = ((), (), s32[]{:S(2)}) async-start(), calls=%async_computation.25 | async-start | bytes 278528 | tf_op jit(solution)/shard_map/reduce_scatter | solution.py:148
  508.1 259.0 %reduce-scatter.22.cloned.1.call-start = ((), (), s32[]{:S(2)}) async-start(), calls=%async_computation.23 | async-start | bytes 278528 | tf_op jit(solution)/shard_map/reduce_scatter | solution.py:142
  508.2 2.5 copy-start.19
  508.2 2.5 copy-start.23
  508.2 2.5 copy-start.24
  511.1 0.9 copy-start.7
  511.1 3.5 copy-start.12
  512.3 0.8 copy-start.17
  512.3 1.0 copy-start.20
  513.3 6.6 collective-permute-start.1
  519.8 309.0 %reduce-scatter.20.cloned.1.call-start = ((), (), s32[]{:S(2)}) async-start(), calls=%async_computation.22 | async-start | bytes 278528 | tf_op jit(solution)/shard_map/reduce_scatter | solution.py:139
  519.9 2.5 copy-start.6
  522.4 0.7 copy-start.10
  524.6 366.1 %reduce-scatter.24.cloned.1.call-start = ((), (), s32[]{:S(2)}) async-start(), calls=%async_computation.24 | async-start | bytes 278528 | tf_op jit(solution)/shard_map/reduce_scatter | solution.py:145
  524.6 3.8 copy-start.8
  529.9 2.0 copy-start.9
  530.0 2.0 copy-start.14
  530.0 439.5 %reduce-scatter.18.cloned.1.call-start = ((), (), s32[]{:S(2)}) async-start(), calls=%async_computation.21 | async-start | bytes 2359296 | tf_op jit(solution)/shard_map/reduce_scatter | solution.py:36
  530.0 2.5 copy-start.2
  534.6 1.3 copy-start.30
  534.6 514.1 %reduce-scatter.14.cloned.1.call-start = ((), (), s32[]{:S(2)}) async-start(), calls=%async_computation.17 | async-start | bytes 2359296 | tf_op jit(solution)/shard_map/reduce_scatter | solution.py:36
  540.4 429.1 %copy-start.26 = (f32[1024]{0:T(1024)S(1)}, f32[1024]{0:T(1024)}, u32[]{:S(2)}) copy-start(f32[1024]{0:T(1024)} %param.13) | copy-start | bytes 12292
  540.4 508.4 %copy-start.11 = (bf16[128,1024]{1,0:T(8,128)(2,1)S(1)}, bf16[128,1024]{1,0:T(8,128)(2,1)}, u32[]{:S(2)}) copy-start(bf16[128,1024]{1,0:T(8,128)(2,1)} %reduce-scatter.16.cloned.1.call-done) | copy-start | bytes 786436
Sparse Core Ops, SparseCore 0:
  11.8 58.3 all-gather.7
  97.3 79.4 reduce-scatter.11
  370.7 75.2 reduce-scatter.15
  449.3 55.4 all-gather.19
Sparse Core Ops, SparseCore 1:
  99.4 36.2 all-gather.13
  179.9 53.6 all-gather.9
  235.1 31.1 all-gather.11
  268.0 32.7 all-gather.15
  303.1 55.2 all-gather.17
  454.3 61.6 reduce-scatter.31
  518.2 61.5 reduce-scatter.29
  582.0 61.2 reduce-scatter.27
  645.5 59.6 reduce-scatter.25
  707.5 59.6 reduce-scatter.21
  769.3 59.5 reduce-scatter.19
  831.2 59.4 reduce-scatter.23
  894.3 75.1 reduce-scatter.17
  973.3 75.4 reduce-scatter.13
where the time goes:
time: 1060 us
  waiting for transfers between devices  795 us (75%)
  blocking collectives  141 us (13%)
  matrix products  66.4 us (6%)
  other arithmetic  26.6 us (3%)
  between operations  16.1 us (2%)
    reduce_scatter x4, waiting for transfers between devices, seq_scatter(): lax.psum_scatter(values.astype(jnp.bfloat16), 'tensor', scatter_dimension...  243 us
    all_gather x4, waiting for transfers between devices, seq_gather(): lax.all_gather(values.astype(jnp.bfloat16), 'tensor', axis=0, tiled=True)  149 us
    psum x1, blocking collectives, per_device(): lax.psum((part_n1, part_n2, placed), ('dp', 'tensor'))  66 us
    reduce_scatter x1, waiting for transfers between devices, per_device(): lax.psum_scatter(g_gate.astype(jnp.bfloat16), 'dp', scatter_dimension=0,...  62 us
    reduce_scatter x1, waiting for transfers between devices, per_device(): lax.psum_scatter(g_c.astype(jnp.bfloat16), 'dp', scatter_dimension=0, til...  60.7 us
    reduce_scatter x1, waiting for transfers between devices, per_device(): lax.psum_scatter(g_x.astype(jnp.bfloat16), 'dp', scatter_dimension=0, til...  60.5 us
    reduce_scatter x1, waiting for transfers between devices, per_device(): lax.psum_scatter(g_b.astype(jnp.bfloat16), 'dp', scatter_dimension=0, til...  60.4 us
    reduce_scatter x1, waiting for transfers between devices, per_device(): lax.psum_scatter(g_out.astype(jnp.bfloat16), 'dp', scatter_dimension=1, t...  60.3 us
  transfers between devices with their start and end apart: 20, of which 16 were waited for; matrix products, arithmetic and copies ran while one was open for 7% of the time, Pallas kernels for 0%

commit v1 on v0

v1 whole, which is shorter than its diff:
```python
import functools

import jax
import jax.numpy as jnp
from jax import lax
from jax.experimental import pallas as pl
from jax.experimental.pallas import tpu as pltpu
from jax.sharding import PartitionSpec as P

SEQ = 2048
OFFSET = 512
EPS = 1e-06
BF = jnp.bfloat16
F32 = jnp.float32
MESH = pl.DeviceIdType.MESH
RING = 4
VMEM_LIMIT = 60 * 1024 * 1024


def tdot(left, right):
    return lax.dot_general(
        left, right, (((0,), (0,)), ((), ())), preferred_element_type=F32
    )


def ndot(left, right):
    return lax.dot_general(
        left, right, (((1,), (1,)), ((), ())), preferred_element_type=F32
    )


def dot(left, right):
    return jnp.dot(left, right, preferred_element_type=F32)


class Place:
    def __init__(self):
        dp, t = lax.axis_index("dp"), lax.axis_index("tensor")
        self.c, self.x = lax.rem(dp, 2), lax.rem(lax.div(dp, 2), RING)
        self.y, self.zhi = lax.div(t, 2), lax.rem(t, 2)
        self.z = self.zhi * 2 + lax.div(dp, 8)

    def at(self, x=None, y=None, z=None, c=None):
        x = self.x if x is None else x
        y = self.y if y is None else y
        z = self.z if z is None else z
        c = self.c if c is None else c
        return (lax.rem(z, 2) * 8 + x * 2 + c, y * 2 + lax.div(z, 2))

    def ring(self, axis):
        p = getattr(self, axis)
        ids = [self.at(**{axis: lax.rem(p + d, RING)}) for d in (1, 3, 2)]
        return (p, *ids)

    def partner(self):
        return self.at(c=1 - self.c)


class Links:
    def __init__(self, send, recv, local=None):
        self.send, self.recv, self.local = send, recv, local
        self.n = 0
        self.m = 0
        self.sent = []

    def push(self, src, dst, dev):
        copy = pltpu.make_async_remote_copy(
            src_ref=src, dst_ref=dst, send_sem=self.send.at[self.n],
            recv_sem=self.recv.at[self.n], device_id=dev, device_id_type=MESH,
        )
        self.n += 1
        copy.start()
        self.sent.append(copy)
        return copy

    def near(self, src, dst):
        copy = pltpu.make_async_copy(src, dst, self.local.at[self.m])
        self.m += 1
        copy.start()
        return copy

    def close(self):
        for copy in self.sent:
            copy.wait_send()


def greet(devs):
    barrier = pltpu.get_barrier_semaphore()
    for dev in devs:
        pl.semaphore_signal(barrier, inc=1, device_id=dev, device_id_type=MESH)
    pl.semaphore_wait(barrier, len(devs))


def ring_gather(links, ring, slot, own=None, arrived=None):
    p, right, left, _ = ring
    own = own or (lambda h: slot(p, h))
    arrived = arrived or (lambda k, h: None)
    r0 = links.push(own(0), slot(p, 0), right)
    l1 = links.push(own(1), slot(p, 1), left)
    r1 = links.push(own(1), slot(p, 1), right)
    l0 = links.push(own(0), slot(p, 0), left)
    before, after, far = lax.rem(p + 3, RING), lax.rem(p + 1, RING), lax.rem(p + 2, RING)
    yield
    r0.wait_recv()
    f0 = links.push(slot(before, 0), slot(before, 0), right)
    arrived(before, 0)
    l1.wait_recv()
    f1 = links.push(slot(after, 1), slot(after, 1), left)
    arrived(after, 1)
    yield
    r1.wait_recv()
    arrived(before, 1)
    l0.wait_recv()
    arrived(after, 0)
    f0.wait_recv()
    arrived(far, 0)
    f1.wait_recv()
    arrived(far, 1)


def ring_reduce(links, ring, part, buf, add, finish):
    p, right, left, _ = ring
    before, after, far = lax.rem(p + 3, RING), lax.rem(p + 1, RING), lax.rem(p + 2, RING)
    a = links.push(part(far, 0), buf[0], right)
    b = links.push(part(far, 1), buf[1], left)
    c = links.push(part(after, 1), buf[2], right)
    d = links.push(part(before, 0), buf[3], left)
    yield
    a.wait_recv()
    add(buf[0], part(after, 0))
    f = links.push(buf[0], buf[4], right)
    b.wait_recv()
    add(buf[1], part(before, 1))
    g = links.push(buf[1], buf[5], left)
    yield
    d.wait_recv()
    f.wait_recv()
    finish(0, part(p, 0), buf[3], buf[4])
    c.wait_recv()
    g.wait_recv()
    finish(1, part(p, 1), buf[2], buf[5])


def drain(gen):
    for _ in gen:
        pass


def rows_of(q):
    return pl.ds(16 * q, 16)


def weight_gather(links, at, full):
    x, z, c = at.x, at.z, at.c
    ring_x, ring_z, mate = at.ring("x"), at.ring("z"), at.partner()
    a1 = ring_gather(links, ring_z, lambda k, h: full.at[:, k, x, c, rows_of(h)])
    b1 = ring_gather(links, ring_x, lambda k, h: full.at[:, z, k, c, rows_of(2 + h)])
    for _ in range(3):
        next(a1, None)
        next(b1, None)
        yield

    crossed = []

    def cross(view):
        crossed.append(links.push(view, view, mate))

    slot_a = lambda k, h: full.at[:, :, k, c, rows_of(h)]
    slot_b = lambda k, h: full.at[:, k, :, c, rows_of(2 + h)]
    a2 = ring_gather(links, ring_x, slot_a, arrived=lambda k, h: cross(slot_a(k, h)))
    b2 = ring_gather(links, ring_z, slot_b, arrived=lambda k, h: cross(slot_b(k, h)))
    next(a2)
    next(b2)
    for h in range(2):
        cross(slot_a(x, h))
        cross(slot_b(z, h))
    yield
    for _ in range(2):
        next(a2, None)
        next(b2, None)
        yield
    for copy in crossed:
        copy.wait_recv()


def add_rows(dst, src):
    if len(dst.shape) == 3:
        for i in range(dst.shape[0]):
            dst[i] = (dst[i].astype(F32) + src[i].astype(F32)).astype(dst.dtype)
        return

    def body(i, _):
        l, k = lax.div(i, RING), lax.rem(i, RING)
        dst[l, k] = (dst[l, k].astype(F32) + src[l, k].astype(F32)).astype(dst.dtype)
        return 0

    lax.fori_loop(0, dst.shape[0] * RING, body, 0)


def weight_reduce(links, at, grads, landed, total, bufs1, bufs2, out):
    x, z, c = at.x, at.z, at.c
    ring_x, ring_z, mate = at.ring("x"), at.ring("z"), at.partner()
    arrays = grads.shape[0]
    swaps = [
        links.push(grads.at[:, k, :, 1 - c], landed.at[:, k], mate) for k in range(RING)
    ]
    yield
    for k in range(RING):
        swaps[k].wait_recv()

        def body(i, _, k=k):
            l, j = lax.div(i, RING), lax.rem(i, RING)
            both = grads[l, k, j, c].astype(F32) + landed[l, k, j].astype(F32)
            total[l, k, j] = both.astype(BF)
            return 0

        lax.fori_loop(0, arrays * RING, body, 0)
    yield

    def finish1(view):
        def run(h, own, one, two):
            def body(i, _):
                l, k = lax.div(i, RING), lax.rem(i, RING)
                s = own[l, k].astype(F32) + one[l, k].astype(F32) + two[l, k].astype(F32)
                own[l, k] = s.astype(BF)
                return 0

            lax.fori_loop(0, arrays * RING, body, 0)

        return run

    part_a = lambda k, h: total.at[:, :, k, rows_of(h)]
    part_b = lambda k, h: total.at[:, k, :, rows_of(2 + h)]
    a1 = ring_reduce(links, ring_x, part_a, [bufs1.at[0, i] for i in range(6)], add_rows, finish1(0))
    b1 = ring_reduce(links, ring_z, part_b, [bufs1.at[1, i] for i in range(6)], add_rows, finish1(1))
    for _ in range(3):
        next(a1, None)
        next(b1, None)
        yield

    def finish2(color):
        def run(h, own, one, two):
            for l in range(arrays):
                s = own[l].astype(F32) + one[l].astype(F32) + two[l].astype(F32)
                out[l, rows_of(2 * color + h)] = s

        return run

    part_a2 = lambda k, h: total.at[:, k, x, rows_of(h)]
    part_b2 = lambda k, h: total.at[:, z, k, rows_of(2 + h)]
    a2 = ring_reduce(links, ring_z, part_a2, [bufs2.at[0, i] for i in range(6)], add_rows, finish2(0))
    b2 = ring_reduce(links, ring_x, part_b2, [bufs2.at[1, i] for i in range(6)], add_rows, finish2(1))
    for _ in range(3):
        next(a2, None)
        next(b2, None)
        yield


def half(ref, k, h):
    return ref.at[k, pl.ds(64 * h, 64)]


def add_tokens(dst, src):
    for i in range(4):
        r = rows_of(i)
        dst[r] = (dst[r].astype(F32) + src[r].astype(F32)).astype(BF)


def call(body, out_shape, out_specs, in_specs, scratch, cid, args):
    return pl.pallas_call(
        body,
        out_shape=out_shape,
        in_specs=in_specs,
        out_specs=out_specs,
        scratch_shapes=scratch,
        compiler_params=pltpu.CompilerParams(
            collective_id=cid, has_side_effects=True, vmem_limit_bytes=VMEM_LIMIT
        ),
    )(*args)


VM = pl.BlockSpec(memory_space=pltpu.VMEM)
ANY = pl.BlockSpec(memory_space=pl.ANY)


def sds(shape, dtype):
    return jax.ShapeDtypeStruct(shape, dtype)


def sems(n):
    return pltpu.SemaphoreType.DMA((n,))


def enter_kernel(
    x_ref, gain_ref, wb, wc, wx, wo, taps_ref,
    h_ref, ob, oc, ox, oo, taps_out,
    full, send, recv, local,
):
    at = Place()
    links = Links(send, recv, local)
    ring_y, ring_x, ring_z = at.ring("y"), at.ring("x"), at.ring("z")
    own = [links.near(w, full.at[i, at.z, at.x, at.c]) for i, w in enumerate((wb, wc, wx, wo))]
    p = at.y
    for i in range(8):
        r = rows_of(i)
        v = x_ref[r]
        r1 = lax.rsqrt(jnp.mean(v * v, -1, keepdims=True) + EPS)
        h_ref[p, r] = (v * r1 * gain_ref[...]).astype(BF)
    taps_out[at.zhi] = taps_ref[...]
    far_z = ring_z[3]
    greet([*ring_y[1:3], *ring_x[1:3], *ring_z[1:4], at.partner()])
    tokens = ring_gather(links, ring_y, lambda k, h: half(h_ref, k, h))
    next(tokens)
    for copy in own:
        copy.wait()
    weights = weight_gather(links, at, full)
    next(weights)
    tap = links.push(taps_ref, taps_out.at[at.zhi], far_z)
    next(weights)
    next(tokens)
    drain(weights)
    outs = []
    for i, o in enumerate((ob, oc, ox, oo)):
        for s in range(2):
            outs.append(
                links.near(full.at[i, pl.ds(2 * s, 2)], o.at[:, :, :, :, pl.ds(128 * s, 128)])
            )
    drain(tokens)
    tap.wait_recv()
    for copy in outs:
        copy.wait()
    links.close()


def enter(block_in, gain, wb, wc, wx, wo, taps):
    w = sds((2, 4, 2, 64, 256), BF)
    return call(
        enter_kernel,
        [sds((RING, 128, 1024), BF), w, w, w, w, sds((2, 3, 128), F32)],
        [VM, ANY, ANY, ANY, ANY, VM],
        [VM, VM, ANY, ANY, ANY, ANY, VM],
        [pltpu.VMEM((4, 4, 4, 2, 64, 128), BF), sems(64), sems(64), sems(16)],
        0,
        (block_in, gain, wb, wc, wx, wo, taps),
    )


def middle_kernel(
    part_ref, x_ref, gain_ref, cot_ref, wg, wu, wd,
    mid_ref, h_ref, cots_ref, g0, g1, u0, u1, d0, d1,
    full, land, send, recv, local,
):
    at = Place()
    links = Links(send, recv, local)
    ring_y, ring_x, ring_z = at.ring("y"), at.ring("x"), at.ring("z")
    own = [links.near(w, full.at[i, at.z, at.x, at.c]) for i, w in enumerate((wg, wu, wd))]
    p = at.y
    greet([*ring_y[1:3], *ring_x[1:3], *ring_z[1:3], at.partner()])

    def finish(h, mine, one, two):
        for i in range(4):
            r = rows_of(i)
            g = pl.ds(64 * h + 16 * i, 16)
            s = mine[r].astype(F32) + one[r].astype(F32) + two[r].astype(F32)
            v = x_ref[g] + s
            mid_ref[g] = v
            r2 = lax.rsqrt(jnp.mean(v * v, -1, keepdims=True) + EPS)
            h_ref[p, g] = (v * r2 * gain_ref[...]).astype(BF)

    reduce = ring_reduce(
        links, ring_y, lambda k, h: half(part_ref, k, h),
        [land.at[i] for i in range(6)], add_tokens, finish,
    )
    next(reduce)
    for copy in own:
        copy.wait()
    weights = weight_gather(links, at, full)
    next(weights)
    for i in range(8):
        r = rows_of(i)
        cots_ref[p, r] = cot_ref[r].astype(BF)
    next(reduce)
    next(weights)
    next(weights)
    next(reduce, None)
    tokens = ring_gather(links, ring_y, lambda k, h: half(h_ref, k, h))
    next(tokens)
    next(weights)
    cots = ring_gather(links, ring_y, lambda k, h: half(cots_ref, k, h))
    next(tokens)
    next(cots)
    next(weights)
    next(cots)
    drain(tokens)
    drain(weights)
    outs = []
    for i, pair in enumerate(((g0, g1), (u0, u1), (d0, d1))):
        for s in range(2):
            outs.append(links.near(full.at[i, pl.ds(2 * s, 2)], pair[s]))
    drain(cots)
    for copy in outs:
        copy.wait()
    links.close()


def middle(part, block_in, gain, cot, wg, wu, wd):
    w = sds((2, 4, 2, 64, 576), BF)
    tokens = sds((RING, 128, 1024), BF)
    return call(
        middle_kernel,
        [sds((128, 1024), F32), tokens, tokens] + [w] * 6,
        [VM, VM, VM] + [ANY] * 6,
        [VM, VM, VM, VM, ANY, ANY, ANY],
        [
            pltpu.VMEM((3, 4, 4, 2, 64, 576), BF), pltpu.VMEM((6, 64, 1024), BF),
            sems(80), sems(80), sems(16),
        ],
        1,
        (part, block_in, gain, cot, wg, wu, wd),
    )


def turn_kernel(
    down_ref, back_ref, mid_ref, gain_ref, cot_ref, g0, g1, u0, u1, d0, d1,
    out_ref, dmid_ref, dmids_ref, norm_ref, grad_ref,
    grads, landed, total, bufs1, bufs2, land, send, recv, local,
):
    at = Place()
    links = Links(send, recv, local)
    ring_y, ring_x, ring_z = at.ring("y"), at.ring("x"), at.ring("z")
    own = []
    for i, pair in enumerate(((g0, g1), (u0, u1), (d0, d1))):
        for s in range(2):
            own.append(links.near(pair[s], grads.at[i, pl.ds(2 * s, 2)]))
    p = at.y
    norm_ref[...] = jnp.zeros_like(norm_ref)
    greet([*ring_y[1:3], *ring_x[1:3], *ring_z[1:3], at.partner()])

    def finish(h, mine, one, two):
        for i in range(4):
            r = rows_of(i)
            g = pl.ds(64 * h + 16 * i, 16)
            dh = mine[r].astype(F32) + one[r].astype(F32) + two[r].astype(F32)
            v = mid_ref[g]
            r2 = lax.rsqrt(jnp.mean(v * v, -1, keepdims=True) + EPS)
            n2 = v * r2
            t = dh * n2
            norm_ref[...] += t[:8] + t[8:]
            dn = dh * gain_ref[...]
            dm = cot_ref[g] + r2 * (dn - n2 * jnp.mean(dn * n2, -1, keepdims=True))
            dmid_ref[g] = dm
            dmids_ref[p, g] = dm.astype(BF)

    def finish_out(h, mine, one, two):
        for i in range(4):
            r = rows_of(i)
            g = pl.ds(64 * h + 16 * i, 16)
            s = mine[r].astype(F32) + one[r].astype(F32) + two[r].astype(F32)
            out_ref[g] = mid_ref[g] + s

    back = ring_reduce(
        links, ring_y, lambda k, h: half(back_ref, k, h),
        [land.at[0, i] for i in range(6)], add_tokens, finish,
    )
    next(back)
    for copy in own:
        copy.wait()
    weights = weight_reduce(links, at, grads, landed, total, bufs1, bufs2, grad_ref)
    next(weights)
    next(back)
    next(weights)
    next(weights)
    next(back, None)
    tokens = ring_gather(links, ring_y, lambda k, h: half(dmids_ref, k, h))
    next(tokens)
    outs = ring_reduce(
        links, ring_y, lambda k, h: half(down_ref, k, h),
        [land.at[1, i] for i in range(6)], add_tokens, finish_out,
    )
    next(weights)
    next(tokens)
    next(outs)
    next(weights)
    next(weights)
    next(outs)
    next(weights)
    drain(tokens)
    drain(outs)
    drain(weights)
    links.close()


def turn(down, back, mid, gain, cot, grads):
    row = sds((128, 1024), F32)
    return call(
        turn_kernel,
        [row, row, sds((RING, 128, 1024), BF), sds((8, 1024), F32), sds((3, 64, 576), F32)],
        [VM] * 5,
        [VM] * 5 + [ANY] * 6,
        [
            pltpu.VMEM((3, 4, 4, 2, 64, 576), BF), pltpu.VMEM((3, 4, 4, 64, 576), BF),
            pltpu.VMEM((3, 4, 4, 64, 576), BF), pltpu.VMEM((2, 6, 3, 4, 16, 576), BF),
            pltpu.VMEM((2, 6, 3, 16, 576), BF), pltpu.VMEM((2, 6, 64, 1024), BF),
            sems(64), sems(64), sems(16),
        ],
        2,
        (down, back, mid, gain, cot, *grads),
    )


def leave_kernel(
    part_ref, x_ref, gain_ref, dmid_ref, small_ref, gb, gc, gx, go,
    gin_ref, grad_ref, sum_ref,
    grads, landed, total, bufs1, bufs2, land, small, send, recv, local,
):
    at = Place()
    links = Links(send, recv, local)
    ring_y, ring_x, ring_z = at.ring("y"), at.ring("x"), at.ring("z")
    own = []
    for i, g in enumerate((gb, gc, gx, go)):
        for s in range(2):
            own.append(
                links.near(g.at[:, :, :, :, pl.ds(128 * s, 128)], grads.at[i, pl.ds(2 * s, 2)])
            )
    greet([*ring_y[1:4], *ring_x[1:4], *ring_z[1:4], at.partner()])
    norm = [jnp.zeros((8, 1024), F32)]

    def finish(h, mine, one, two):
        for i in range(4):
            r = rows_of(i)
            g = pl.ds(64 * h + 16 * i, 16)
            dh = mine[r].astype(F32) + one[r].astype(F32) + two[r].astype(F32)
            v = x_ref[g]
            r1 = lax.rsqrt(jnp.mean(v * v, -1, keepdims=True) + EPS)
            n1 = v * r1
            t = dh * n1
            norm[0] = norm[0] + t[:8] + t[8:]
            dn = dh * gain_ref[...]
            gin_ref[g] = dmid_ref[g] + r1 * (dn - n1 * jnp.mean(dn * n1, -1, keepdims=True))

    back = ring_reduce(
        links, ring_y, lambda k, h: half(part_ref, k, h),
        [land.at[i] for i in range(6)], add_tokens, finish,
    )
    next(back)
    for copy in own:
        copy.wait()
    weights = weight_reduce(links, at, grads, landed, total, bufs1, bufs2, grad_ref)
    next(weights)
    next(back)
    next(weights)
    next(weights)
    next(back, None)
    first = lax.broadcasted_iota(jnp.int32, (8, 1024), 0) == 0
    total_norm = jnp.sum(norm[0], 0, keepdims=True)
    value = small_ref[...] + jnp.where(first, total_norm, 0.0)
    stages = (("y", ring_y), ("x", ring_x), ("z", ring_z))
    for s, (axis, ring) in enumerate(stages):
        pos = ring[0]
        small[s, pos] = value
        copies = [links.push(small.at[s, pos], small.at[s, pos], dev) for dev in ring[1:4]]
        next(weights, None)
        for copy in copies:
            copy.wait_recv()
        value = (small[s, 0] + small[s, 1]) + (small[s, 2] + small[s, 3])
    small[3, at.c] = value
    copy = links.push(small.at[3, at.c], small.at[3, at.c], at.partner())
    next(weights, None)
    copy.wait_recv()
    sum_ref[...] = small[3, 0] + small[3, 1]
    drain(weights)
    links.close()


def leave(part, block_in, gain, dmid, small, grads):
    return call(
        leave_kernel,
        [sds((128, 1024), F32), sds((4, 64, 128), F32), sds((8, 1024), F32)],
        [VM] * 3,
        [VM] * 5 + [ANY] * 4,
        [
            pltpu.VMEM((4, 4, 4, 2, 64, 128), BF), pltpu.VMEM((4, 4, 4, 64, 128), BF),
            pltpu.VMEM((4, 4, 4, 64, 128), BF), pltpu.VMEM((2, 6, 4, 4, 16, 128), BF),
            pltpu.VMEM((2, 6, 4, 16, 128), BF), pltpu.VMEM((6, 64, 1024), BF),
            pltpu.VMEM((4, 4, 8, 1024), F32), sems(64), sems(64), sems(16),
        ],
        3,
        (part, block_in, gain, dmid, small, *grads),
    )


def halo_routes(n_dp, step):
    swap = [(d * 8 + t, d * 8 + (t ^ 1)) for d in range(n_dp) for t in range(8)]
    if step > 0:
        cross = [(d * 8 + t, d * 8 + 8 + t - 1) for d in range(n_dp - 1) for t in (1, 3, 5, 7)]
    else:
        cross = [(d * 8 + t, d * 8 - 8 + t + 1) for d in range(1, n_dp) for t in (0, 2, 4, 6)]
    return swap, cross


def per_device(
    block_in, norm1_gain, w_b, w_c, w_x, conv_w, w_out, norm2_gain, w_gate, w_up, w_down, out_cot
):
    axes = ("dp", "tensor")
    dp, t = lax.axis_index("dp"), lax.axis_index("tensor")
    n_dp = lax.axis_size("dp")
    zhi = t % 2
    gain1, gain2 = norm1_gain[None, :], norm2_gain[None, :]
    h1, wb, wc, wx, wo, taps = enter(block_in, gain1, w_b, w_c, w_x, w_out.T, conv_w)
    wb, wc, wx, wo = (w.reshape(1024, 256) for w in (wb, wc, wx, wo))
    taps = taps.transpose(1, 0, 2).reshape(3, 256)
    h1 = h1.reshape(512, 1024)
    block = dp * 8 + 2 * jnp.arange(RING, dtype=jnp.int32) + zhi
    begins = lambda r: (r == 0) | ((r * 128 + SEQ - OFFSET) % SEQ == 0)
    keep_back = jnp.where(begins(block), 0.0, 1.0).astype(F32)[:, None, None]
    following = block + 1
    keep_fwd = jnp.where(
        begins(following) | (following == n_dp * 8), 0.0, 1.0
    ).astype(F32)[:, None, None]

    bproj, xproj = dot(h1, wb), dot(h1, wx)
    gated = (bproj * xproj).reshape(RING, 128, 256)
    swap, cross = halo_routes(n_dp, 1)
    tails = gated[:, -2:]
    near = lax.ppermute(tails, axes, swap)
    wrap = lax.ppermute(tails[-1:], axes, cross)
    cproj = dot(h1, wc).reshape(RING, 128, 256)
    shifted = jnp.concatenate([wrap, near[:-1]], 0)
    halo = jnp.where(zhi == 1, near, shifted) * keep_back
    extended = jnp.concatenate([halo, gated], 1)
    two, one = extended[:, :-2], extended[:, 1:-1]
    conv = taps[0] * two + taps[1] * one + taps[2] * gated
    ymix = (cproj * conv).astype(BF).reshape(512, 256)
    part = ndot(ymix, wo).astype(BF).reshape(RING, 128, 1024)
    mid, h2, cots, *ffn = middle(part, block_in, gain2, out_cot, w_gate, w_up, w_down.T)
    wg, wu, wd = ([w.reshape(1024, 576) for w in ffn[2 * i : 2 * i + 2]] for i in range(3))
    h2, cots = h2.reshape(512, 1024), cots.reshape(512, 1024)
    down, back = 0.0, 0.0
    g_gate, g_up, g_down = [], [], []
    for s in range(2):
        gate, up = dot(h2, wg[s]), dot(h2, wu[s])
        sig = jax.nn.sigmoid(gate)
        act = (gate * sig * up).astype(BF)
        dact = dot(cots, wd[s])
        dgate = (dact * up * sig * (1.0 + gate * (1.0 - sig))).astype(BF)
        dup = (dact * gate * sig).astype(BF)
        down = down + ndot(act, wd[s])
        back = back + ndot(dgate, wg[s]) + ndot(dup, wu[s])
        split = lambda g: g.astype(BF).reshape(2, 4, 2, 64, 576)
        g_gate.append(split(tdot(h2, dgate)))
        g_up.append(split(tdot(h2, dup)))
        g_down.append(split(tdot(cots, act)))
    tokens = lambda v: v.astype(BF).reshape(RING, 128, 1024)
    block_out, dmid, dmids, sums2, ffn_grads = turn(
        tokens(down), tokens(back), mid, gain2, out_cot, (*g_gate, *g_up, *g_down)
    )
    dmids = dmids.reshape(512, 1024)
    dy = dot(dmids, wo)
    dy = dy.reshape(RING, 128, 256)
    dconv = dy * cproj
    swap, cross = halo_routes(n_dp, -1)
    heads = dconv[:, :2]
    near = lax.ppermute(heads, axes, swap)
    wrap = lax.ppermute(heads[:1], axes, cross)
    g_out = tdot(dmids, ymix)
    dc = (dy * conv).astype(BF).reshape(512, 256)
    shifted = jnp.concatenate([near[1:], wrap], 0)
    halo = jnp.where(zhi == 0, near, shifted) * keep_fwd
    after = jnp.concatenate([dconv, halo], 1)
    dgated = taps[2] * dconv + taps[1] * after[:, 1:-1] + taps[0] * after[:, 2:]
    dgated = dgated.reshape(512, 256)
    part_conv = jnp.stack(
        [jnp.sum(dconv * v, (0, 1)) for v in (two, one, gated)], 0
    )
    db = (dgated * xproj).astype(BF)
    dx = (dgated * bproj).astype(BF)
    part1 = tokens(ndot(db, wb) + ndot(dc, wc) + ndot(dx, wx))
    split = lambda g: g.astype(BF).reshape(2, 4, 2, 64, 256)
    small = jnp.zeros((8, 1024), F32)
    small = small.at[1].set(jnp.sum(sums2, 0))
    small = lax.dynamic_update_slice(small, part_conv, (jnp.int32(2), (t // 2) * 256))
    grad_in, mix_grads, total = leave(
        part1, block_in, gain1, dmid, small,
        (split(tdot(h1, db)), split(tdot(h1, dc)), split(tdot(h1, dx)), split(g_out)),
    )
    grad_conv = lax.dynamic_slice(total, (jnp.int32(2), t * 128), (3, 128))
    return (
        block_out, grad_in, total[0], mix_grads[0], mix_grads[1], mix_grads[2], grad_conv,
        mix_grads[3].T, total[1], ffn_grads[0], ffn_grads[1], ffn_grads[2].T,
    )


def solution(mesh):
    tok, mat, tam = P(("dp", "tensor"), None), P("dp", "tensor"), P("tensor", "dp")
    taps = P(None, "tensor")
    return jax.shard_map(
        per_device,
        mesh=mesh,
        in_specs=(tok, P(), mat, mat, mat, taps, tam, P(), mat, mat, tam, tok),
        out_specs=(tok, tok, P(), mat, mat, mat, taps, tam, P(), mat, mat, tam),
        check_vma=False,
    )
```

time: 1060 us -> 235 us (0.22)
  waiting for transfers between devices: 795 us -> 2.63 us
  Pallas kernels: 0 us -> 148 us
  blocking collectives: 141 us -> 0 us
  other arithmetic: 26.6 us -> 0.74 us
  local copies, waits for them, and re-layouts: 8.83 us -> 26.4 us
  matrix products: 66.4 us -> 50.3 us
  between operations: 16.1 us -> 1.16 us
    reduce_scatter x11 -> x0, waiting for transfers between devices: 585 us -> none  [the longest x4 243 us: seq_scatter(): lax.psum_scatter(values.astype(jnp.bfloat16), 'tensor', scatter_dimension...]
    all_gather x7 -> x0, waiting for transfers between devices: 207 us -> none  [the longest x4 149 us: seq_gather(): lax.all_gather(values.astype(jnp.bfloat16), 'tensor', axis=0, tiled=True)]
    pallas_call x0 -> x4, Pallas kernels: none -> 148 us  [call(): pl.pallas_call(body, out_shape=out_shape, in_specs=in_specs, out_specs=ou...]
    all_gather x4 -> x0, blocking collectives: 75 us -> none  [the longest x1 21.1 us: per_device(): lax.all_gather(w_b, 'dp', axis=0, tiled=True)]
    psum x1 -> x0, blocking collectives: 66 us -> none  [per_device(): lax.psum((part_n1, part_n2, placed), ('dp', 'tensor'))]
    convert_element_type x13 -> x1, other arithmetic: 18.8 us -> 0.11 us  [per_device(): dx = (dgated * bproj).astype(BF)]
    convert_element_type x0 -> x6, local copies, waits for them, and re-layouts: none -> 14.6 us  [per_device(): split = lambda g: g.astype(BF).reshape(2, 4, 2, 64, 576)]
    dot_general x7 -> x10, matrix products: 21.8 us -> 14.8 us  [dot(): return jnp.dot(left, right, preferred_element_type=F32)]
  transfers between devices with their start and end apart: 20 -> 4, of which waited for: 16 -> 1; matrix products, arithmetic and copies ran while one was open for 7% -> 1% of each run, Pallas kernels for 0% -> 0%
where the time goes in v1:
time: 235 us; the launch traced here: 234 us
  Pallas kernels  148 us (63%)
  matrix products  50.3 us (21%)
  local copies, waits for them, and re-layouts  26.4 us (11%)
  starting transfers between devices  4.72 us (2%)
  waiting for transfers between devices  2.63 us (1%)
    pallas_call x4, Pallas kernels, call(): pl.pallas_call(body, out_shape=out_shape, in_specs=in_specs, out_specs=ou...  148 us
    dot_general x10, matrix products, tdot(): lax.dot_general(left, right, (((0,), (0,)), ((), ())), preferred_element_...  17.8 us
    dot_general x10, matrix products, ndot(): lax.dot_general(left, right, (((1,), (1,)), ((), ())), preferred_element_...  17.7 us
    dot_general x10, matrix products, dot(): return jnp.dot(left, right, preferred_element_type=F32)  14.8 us
    convert_element_type x6, local copies, waits for them, and re-layouts, per_device(): split = lambda g: g.astype(BF).reshape(2, 4, 2, 64, 576)  14.6 us
    unnamed x62, local copies, waits for them, and re-layouts  6.4 us
  transfers between devices with their start and end apart: 4, of which 1 were waited for; matrix products, arithmetic and copies ran while one was open for 1% of the time, Pallas kernels for 0%

profile of v1, /device:TPU:0, one launch (start us, length us, event | category | flops | bytes accessed | tf_op | source)
XLA Modules:
  0.0 234.0 jit_solution(14919331813012585485)
XLA Ops:
  0.6 26.7 %shard_map.211 = (bf16[4,128,1024]{2,1,0:T(8,128)(2,1)}, bf16[2,4,2,64,256]{4,3,2,1,0:T(8,128)(2,1)}, bf16[2,4,2,64,256]{4,3,2,1,0:T(8,128)(2,1)}, bf16[2,4,2,64...) custom-call(f32[128,1024]{1,0:T(8,128)} %x_ref.5, f32[1,1024]{1,0:T(1,128)} %bitcast.189, ...), custom_call_target="tpu_custom_call" | custom-call | tf_op jit(solution)/shard_map/pallas_call | solution.py:270
  27.4 1.9 fusion.17
  29.4 1.2 fusion.16
  30.6 1.8 collective-permute-start
  32.4 0.6 collective-permute-start.1
  33.1 2.6 %collective-permute-done = f32[4,2,256]{2,1,0:T(2,128)S(1)} collective-permute-done((f32[4,2,256]{2,1,0:T(2,128)S(1)}, f32[4,2,256]{2,1,0:T(2,128)S(1)}, u32[]{:S(2)}, u32[]{:S(2)}) %collective-permute-start) | collective-permute-done | bytes 8224 | tf_op jit(solution)/shard_map/ppermute | solution.py:625
  35.8 1.4 multiply_convert_fusion.7
  37.3 1.5 convolution_convert_fusion.6
  38.8 44.0 %shard_map.212 = (f32[128,1024]{1,0:T(8,128)}, bf16[4,128,1024]{2,1,0:T(8,128)(2,1)}, bf16[4,128,1024]{2,1,0:T(8,128)(2,1)}, bf16[2,4,2,64,576]{4,3,2,1,0:T(8,12...) custom-call(bf16[4,128,1024]{2,1,0:T(8,128)(2,1)} %bitcast.158, ...), custom_call_target="tpu_custom_call" | custom-call | tf_op jit(solution)/shard_map/pallas_call | solution.py:270
  82.9 2.6 %fusion.18 = f32[512,576]{0,1:T(8,128)S(1)} fusion(bf16[512,1024]{1,0:T(8,128)(2,1)} %bitcast.205, bf16[1024,576]{1,0:T(8,128)(2,1)} %bitcast.174), kind=kOutput, calls=%fused_computation.74 | convolution fusion | flops 603979776 | bytes 3407872 | tf_op jit(solution)/shard_map/dot_general | solution.py:33
  85.5 0.8 fusion.19
  86.4 0.5 copy-done.12
  86.8 0.3 copy-done.29
  87.1 1.3 multiply_convert_fusion.2
  88.4 1.0 fusion.23
  89.5 1.8 convolution_convert_fusion.5
  91.3 0.8 fusion.21
  92.2 0.5 copy-done.11
  92.7 0.8 fusion.22
  93.5 0.5 copy-done.16
  94.0 2.1 multiply_convert_fusion
  96.1 2.4 %fusion.25 = f32[512,1024]{1,0:T(8,128)} fusion(bf16[512,576]{0,1:T(8,128)(2,1)S(1)} %get-tuple-element.77, bf16[1024,576]{1,0:T(8,128)(2,1)S(1)} %bitcast.173), kind=kOutput, calls=%fused_computation.81 | convolution fusion | flops 603979776 | bytes 3866624 | tf_op jit(solution)/shard_map/dot_general | solution.py:27
  98.5 1.9 convolution_convert_fusion.4
  100.4 2.4 %fusion.24 = f32[512,1024]{1,0:T(8,128)} fusion(bf16[512,576]{0,1:T(8,128)(2,1)S(1)} %get-tuple-element.79, bf16[1024,576]{1,0:T(8,128)(2,1)S(1)} %bitcast.171), kind=kOutput, calls=%fused_computation.80 | convolution fusion | flops 603979776 | bytes 3866624 | tf_op jit(solution)/shard_map/dot_general | solution.py:27
  102.7 2.0 convolution_convert_fusion.3
  104.7 1.0 fusion.20
  105.8 1.9 convolution_convert_fusion.1
  107.7 1.8 convolution_convert_fusion
  109.4 2.1 add_convert_fusion.2
  111.5 2.4 %copy.24 = bf16[1024,576]{1,0:T(8,128)(2,1)} copy(bf16[1024,576]{0,1:T(8,128)(2,1)} %convolution_convert_fusion.5) | data formatting | bytes 2359296 | tf_op jit(solution)/shard_map/convert_element_type | solution.py:649
  113.9 2.5 %copy.25 = bf16[1024,576]{1,0:T(8,128)(2,1)} copy(bf16[1024,576]{0,1:T(8,128)(2,1)} %convolution_convert_fusion.4) | data formatting | bytes 2359296 | tf_op jit(solution)/shard_map/convert_element_type | solution.py:649
  116.4 2.5 %copy.26 = bf16[1024,576]{1,0:T(8,128)(2,1)} copy(bf16[1024,576]{0,1:T(8,128)(2,1)} %convolution_convert_fusion.3) | data formatting | bytes 2359296 | tf_op jit(solution)/shard_map/convert_element_type | solution.py:649
  118.8 3.2 %convolution_convert_fusion.2 = bf16[1024,576]{0,1:T(8,128)(2,1)} fusion(bf16[512,576]{0,1:T(8,128)(2,1)} %get-tuple-element.76, bf16[512,1024]{1,0:T(8,128)(2,1)} %bitcast.206), kind=kOutput, calls=%fused_computation.5 | convolution fusion | flops 604569600 | bytes 2818048 | tf_op jit(solution)/shard_map/dot_general | solution.py:21
  122.0 2.4 %copy.27 = bf16[1024,576]{1,0:T(8,128)(2,1)} copy(bf16[1024,576]{0,1:T(8,128)(2,1)} %convolution_convert_fusion.2) | data formatting | bytes 2359296 | tf_op jit(solution)/shard_map/convert_element_type | solution.py:649
  124.4 2.4 %copy.28 = bf16[1024,576]{1,0:T(8,128)(2,1)} copy(bf16[1024,576]{0,1:T(8,128)(2,1)} %convolution_convert_fusion.1) | data formatting | bytes 2359296 | tf_op jit(solution)/shard_map/convert_element_type | solution.py:649
  126.8 2.4 %copy.29 = bf16[1024,576]{1,0:T(8,128)(2,1)} copy(bf16[1024,576]{0,1:T(8,128)(2,1)} %convolution_convert_fusion) | data formatting | bytes 2359296 | tf_op jit(solution)/shard_map/convert_element_type | solution.py:649
  129.3 4.9 %add_convert_fusion.1 = bf16[512,1024]{1,0:T(8,128)(2,1)} fusion(f32[512,1024]{1,0:T(8,128)} %fusion.25, f32[512,1024]{1,0:T(8,128)S(1)} %fusion.23, f32[512,1024]{1,0:T(8,128)} %fusion.24, bf16[512,576]{0,1:T(8,128)(2,1)} %get-tuple-element.76, bf16[1024,576]{1,0:T(8,128)(2,1)} %bitcast.166), kind=kOutput, calls=%fused_computation.1 | convolution fusion | flops 606076928 | bytes 9109504 | tf_op jit(solution)/shard_map/dot_general | solution.py:27
  134.1 41.7 %shard_map.213 = (f32[128,1024]{1,0:T(8,128)}, f32[128,1024]{1,0:T(8,128)}, bf16[4,128,1024]{2,1,0:T(8,128)(2,1)}, f32[8,1024]{1,0:T(8,128)}, f32[3,64,576]{2,1,0:T(8,128)}) custom-call(bf16[4,128,1024]{2,1,0:T(8,128)(2,1)} %bitcast.152, bf16[4,128,1024]{2,1,0:T(8,128)(2,1)} %bitcast.153, f32[128,1024]{1,0:T(8,128)} %get-tuple-element.61.mid_ref, ...), custom_call_target="tpu_custom_call" | custom-call | tf_op jit(solution)/shard_map/pallas_call | solution.py:270
  175.8 1.7 fusion.26
  177.6 0.3 multiply_reduce_fusion.2
  177.9 1.0 copy-done.17
  178.9 1.3 fusion.1
  180.2 1.5 collective-permute-start.2
  181.7 0.9 collective-permute-start.3
  182.6 1.3 fusion
  183.9 0.8 slice_bitcast_fusion
  184.7 0.5 fusion.28
  185.2 0.3 copy-done.26
  185.5 0.4 dynamic_update_slice.3.small_ref
  186.1 0.2 fusion.5
  186.2 0.8 copy-done.10
  187.0 0.1 fusion.9
  187.1 0.2 copy-done.9
  187.3 0.5 fusion.27
  187.8 0.8 copy-done.2
  188.5 1.3 convolution_convert_fusion.8
  189.8 1.3 convolution_convert_fusion.7
  191.1 1.5 add_convert_fusion
  192.6 35.6 %shard_map.214 = (f32[128,1024]{1,0:T(8,128)}, f32[4,64,128]{2,1,0:T(8,128)}, f32[8,1024]{1,0:T(8,128)}) custom-call(bf16[4,128,1024]{2,1,0:T(8,128)(2,1)} %bitcast.159, f32[128,1024]{1,0:T(8,128)} %x_ref.5, f32[1,1024]{1,0:T(1,128)} %bitcast.190, f32[128,1024]{1,0:T(8,128)} %get-tuple-element.64.dmid_ref, f32[8,1024]{1,0:T(8,128)} %copy-done.25, ...), custom_call_target="tpu_custom_call" | custom-call | tf_op jit(solution)/shard_map/pallas_call | solution.py:270
  228.2 1.4 fusion.14
  229.7 1.5 slice_bitcast_fusion.3
  231.1 1.3 constant_dynamic-slice_fusion
  232.4 0.8 copy.37
  233.2 0.8 copy.38
  (68 shorter events, 0.4 us)
Async XLA Ops:
  27.4 1.9 copy-start
  27.4 1.9 copy-start.8
  29.3 3.7 %copy-start.27 = (f32[2,3,128]{2,1,0:T(4,128)S(1)}, f32[2,3,128]{2,1,0:T(4,128)}, u32[]{:S(2)}) copy-start(f32[2,3,128]{2,1,0:T(4,128)} %get-tuple-element.49) | copy-start | bytes 9220
  29.3 6.5 %copy-start.20 = (bf16[2,4,2,64,256]{4,3,2,1,0:T(8,128)(2,1)S(1)}, bf16[2,4,2,64,256]{4,3,2,1,0:T(8,128)(2,1)}, u32[]{:S(2)}) copy-start(bf16[2,4,2,64,256]{4,3,2,1,0:T(8,128)(2,1)} %get-tuple-element.48) | copy-start | bytes 1572868
  30.6 5.2 %collective-permute-start = (f32[4,2,256]{2,1,0:T(2,128)S(1)}, f32[4,2,256]{2,1,0:T(2,128)S(1)}, u32[]{:S(2)}, u32[]{:S(2)}) collective-permute-start(f32[4,2,256]{2,1,0:T(2,128)S(1)} %slice.111), channel_id=1, source_target_pairs={{0,1},{1,0},{2,3},{3,2},{4,5},{5,4},{6,7},{7,6},{8,9},{9,8},{10,11... | collective-permute-start | bytes 24584 | tf_op jit(solution)/shard_map/ppermute | solution.py:625
  32.4 3.4 %collective-permute-start.1 = (f32[1,2,256]{2,1,0:T(2,128)S(1)}, f32[1,2,256]{2,1,0:T(2,128)S(1)}, u32[]{:S(2)}, u32[]{:S(2)}) collective-permute-start(f32[1,2,256]{2,1,0:T(2,128)S(1)} %slice.112), channel_id=1, source_target_pairs={{1,8},{3,10},{5,12},{7,14},{9,16},{11,18},{13,20},{15,22},{17,24},... | collective-permute-start | bytes 6152 | tf_op jit(solution)/shard_map/ppermute | solution.py:626
  35.8 1.4 copy-start.6
  82.9 2.6 %copy-start.13 = (bf16[2,4,2,64,576]{4,3,2,1,0:T(8,128)(2,1)S(1)}, bf16[2,4,2,64,576]{4,3,2,1,0:T(8,128)(2,1)}, u32[]{:S(2)}) copy-start(bf16[2,4,2,64,576]{4,3,2,1,0:T(8,128)(2,1)} %get-tuple-element.55) | copy-start | bytes 3538948
  82.9 2.6 %copy-start.28 = (bf16[4,128,1024]{2,1,0:T(8,128)(2,1)S(1)}, bf16[4,128,1024]{2,1,0:T(8,128)(2,1)}, u32[]{:S(2)}) copy-start(bf16[4,128,1024]{2,1,0:T(8,128)(2,1)} %get-tuple-element.53) | copy-start | bytes 3145732
  85.5 1.3 copy-start.12
  85.5 1.6 copy-start.29
  87.1 1.3 copy-start.15
  89.5 1.8 copy-start.14
  91.3 1.3 copy-start.11
  92.7 1.3 copy-start.16
  134.1 41.7 %copy-start.7 = (bf16[2,4,2,64,256]{4,3,2,1,0:T(8,128)(2,1)S(1)}, bf16[2,4,2,64,256]{4,3,2,1,0:T(8,128)(2,1)}, u32[]{:S(2)}) copy-start(bf16[2,4,2,64,256]{4,3,2,1,0:T(8,128)(2,1)} %get-tuple-element.52) | copy-start | bytes 1572868
  175.8 1.8 copy-start.22
  175.8 1.8 copy-start.23
  177.6 1.3 copy-start.17
  177.9 6.0 %copy-start.3 = (f32[4,128,256]{2,1,0:T(8,128)}, f32[4,128,256]{2,1,0:T(8,128)S(1)}, u32[]{:S(2)}) copy-start(f32[4,128,256]{2,1,0:T(8,128)S(1)} %get-tuple-element.73) | copy-start | bytes 1572868
  177.9 4.7 %copy-start.1 = (bf16[4,128,1024]{2,1,0:T(8,128)(2,1)S(1)}, bf16[4,128,1024]{2,1,0:T(8,128)(2,1)}, u32[]{:S(2)}) copy-start(bf16[4,128,1024]{2,1,0:T(8,128)(2,1)} %get-tuple-element.47) | copy-start | bytes 3145732
  180.2 3.7 %copy-start.24 = (f32[3,64,576]{2,1,0:T(8,128)S(1)}, f32[3,64,576]{2,1,0:T(8,128)}, u32[]{:S(2)}) copy-start(f32[3,64,576]{2,1,0:T(8,128)} %get-tuple-element.69) | copy-start | bytes 1327108
  180.2 5.7 %collective-permute-start.2 = (f32[4,2,256]{2,1,0:T(2,128)S(1)}, f32[4,2,256]{2,1,0:T(2,128)S(1)}, u32[]{:S(2)}, u32[]{:S(2)}) collective-permute-start(f32[4,2,256]{2,1,0:T(2,128)S(1)} %slice.118), channel_id=1, source_target_pairs={{0,1},{1,0},{2,3},{3,2},{4,5},{5,4},{6,7},{7,6},{8,9},{9,8},{10,11... | collective-permute-start | bytes 24584 | tf_op jit(solution)/shard_map/ppermute | solution.py:663
  181.7 4.3 %collective-permute-start.3 = (f32[1,2,256]{2,1,0:T(2,128)S(1)}, f32[1,2,256]{2,1,0:T(2,128)S(1)}, u32[]{:S(2)}, u32[]{:S(2)}) collective-permute-start(f32[1,2,256]{2,1,0:T(2,128)S(1)} %slice.120), channel_id=1, source_target_pairs={{8,1},{10,3},{12,5},{14,7},{16,9},{18,11},{20,13},{22,15},{24,17},... | collective-permute-start | bytes 6152 | tf_op jit(solution)/shard_map/ppermute | solution.py:664
  182.6 2.1 copy-start.21
  184.7 0.8 copy-start.26
  184.7 1.4 copy-start.4
  185.9 1.2 copy-start.25
  185.9 1.1 copy-start.10
  186.2 1.1 copy-start.9
  187.3 1.2 copy-start.2
  189.8 1.3 copy-start.5
  192.6 39.8 %copy-start.18 = (f32[128,1024]{1,0:T(8,128)S(1)}, f32[128,1024]{1,0:T(8,128)}, u32[]{:S(2)}) copy-start(f32[128,1024]{1,0:T(8,128)} %get-tuple-element.112) | copy-start | bytes 1572868
  228.2 5.0 %copy-start.19 = (f32[128,1024]{1,0:T(8,128)S(1)}, f32[128,1024]{1,0:T(8,128)}, u32[]{:S(2)}) copy-start(f32[128,1024]{1,0:T(8,128)} %get-tuple-element.113) | copy-start | bytes 1572868

commit v2 on v0

v2 whole, which is shorter than its diff:
```python
import jax
import jax.numpy as jnp
from jax import lax
from jax.experimental import pallas as pl
from jax.experimental.pallas import tpu as pltpu
from jax.sharding import PartitionSpec as P

SEQ = 2048
OFFSET = 512
EPS = 1e-06
BF = jnp.bfloat16
F32 = jnp.float32
MESH = pl.DeviceIdType.MESH
RING = 4
VMEM_LIMIT = 63 * 1024 * 1024


def tdot(left, right):
    return lax.dot_general(
        left, right, (((0,), (0,)), ((), ())), preferred_element_type=F32
    )


def ndot(left, right):
    return lax.dot_general(
        left, right, (((1,), (1,)), ((), ())), preferred_element_type=F32
    )


def dot(left, right):
    return jnp.dot(left, right, preferred_element_type=F32)


class Place:
    def __init__(self):
        dp, t = lax.axis_index("dp"), lax.axis_index("tensor")
        self.c, self.x = lax.rem(dp, 2), lax.rem(lax.div(dp, 2), RING)
        self.y, self.zhi = lax.div(t, 2), lax.rem(t, 2)
        self.z = self.zhi * 2 + lax.div(dp, 8)

    def at(self, x=None, y=None, z=None, c=None):
        x = self.x if x is None else x
        y = self.y if y is None else y
        z = self.z if z is None else z
        c = self.c if c is None else c
        return (lax.rem(z, 2) * 8 + x * 2 + c, y * 2 + lax.div(z, 2))

    def ring(self, axis):
        p = getattr(self, axis)
        ids = [self.at(**{axis: lax.rem(p + d, RING)}) for d in (1, 3, 2)]
        return (p, *ids)

    def partner(self):
        return self.at(c=1 - self.c)


class Links:
    def __init__(self, send, recv, local=None):
        self.send, self.recv, self.local = send, recv, local
        self.n = 0
        self.m = 0
        self.sent = []

    def push(self, src, dst, dev):
        copy = pltpu.make_async_remote_copy(
            src_ref=src, dst_ref=dst, send_sem=self.send.at[self.n],
            recv_sem=self.recv.at[self.n], device_id=dev, device_id_type=MESH,
        )
        self.n += 1
        copy.start()
        self.sent.append(copy)
        return copy

    def near(self, src, dst):
        copy = pltpu.make_async_copy(src, dst, self.local.at[self.m])
        self.m += 1
        copy.start()
        return copy

    def close(self):
        for copy in self.sent:
            copy.wait_send()


def greet(devs):
    barrier = pltpu.get_barrier_semaphore()
    for dev in devs:
        pl.semaphore_signal(barrier, inc=1, device_id=dev, device_id_type=MESH)
    pl.semaphore_wait(barrier, len(devs))


def around(p):
    return lax.rem(p + 3, RING), lax.rem(p + 1, RING), lax.rem(p + 2, RING)


def ring_gather(links, ring, slot, arrived=None, staged=False):
    p, right, left, _ = ring
    before, after, far = around(p)
    arrived = arrived or (lambda k, h: None)
    r0 = links.push(slot(p, 0), slot(p, 0), right)
    if staged:
        l0 = links.push(slot(p, 0), slot(p, 0), left)
        yield
    l1 = links.push(slot(p, 1), slot(p, 1), left)
    r1 = links.push(slot(p, 1), slot(p, 1), right)
    if not staged:
        l0 = links.push(slot(p, 0), slot(p, 0), left)
    yield
    r0.wait_recv()
    f0 = links.push(slot(before, 0), slot(before, 0), right)
    arrived(before, 0)
    l1.wait_recv()
    f1 = links.push(slot(after, 1), slot(after, 1), left)
    arrived(after, 1)
    yield
    r1.wait_recv()
    arrived(before, 1)
    l0.wait_recv()
    arrived(after, 0)
    f0.wait_recv()
    arrived(far, 0)
    f1.wait_recv()
    arrived(far, 1)


def ring_reduce(links, ring, part, buf, add, staged=False):
    p, right, left, _ = ring
    before, after, far = around(p)
    a = links.push(part(far, 0), buf[0], right)
    if staged:
        d = links.push(part(before, 0), buf[3], left)
        yield
    b = links.push(part(far, 1), buf[1], left)
    c = links.push(part(after, 1), buf[2], right)
    if not staged:
        d = links.push(part(before, 0), buf[3], left)
    yield
    a.wait_recv()
    add(buf[0], part(after, 0))
    f = links.push(buf[0], buf[4], right)
    b.wait_recv()
    add(buf[1], part(before, 1))
    g = links.push(buf[1], buf[5], left)
    yield
    for copy in (c, d, f, g):
        copy.wait_recv()


def drain(gen):
    for _ in gen:
        pass


def rows_of(q):
    return pl.ds(16 * q, 16)


def weight_gather(links, at, full):
    x, z, c = at.x, at.z, at.c
    ring_x, ring_z, mate = at.ring("x"), at.ring("z"), at.partner()
    a1 = ring_gather(links, ring_z, lambda k, h: full.at[:, k, x, c, rows_of(h)])
    b1 = ring_gather(links, ring_x, lambda k, h: full.at[:, z, k, c, rows_of(2 + h)])
    for i in range(3):
        next(a1, None)
        next(b1, None)
        if i < 2:
            yield

    crossed = []

    def cross(view):
        crossed.append(links.push(view, view, mate))

    slot_a = lambda k, h: full.at[:, :, k, c, rows_of(h)]
    slot_b = lambda k, h: full.at[:, k, :, c, rows_of(2 + h)]
    a2 = ring_gather(links, ring_x, slot_a, arrived=lambda k, h: cross(slot_a(k, h)))
    b2 = ring_gather(links, ring_z, slot_b, arrived=lambda k, h: cross(slot_b(k, h)))
    next(a2)
    next(b2)
    for h in range(2):
        cross(slot_a(x, h))
        cross(slot_b(z, h))
    yield
    for _ in range(2):
        next(a2, None)
        next(b2, None)
        yield
    for copy in crossed:
        copy.wait_recv()


def plus(*terms):
    total = terms[0].astype(F32)
    for t in terms[1:]:
        total = total + t.astype(F32)
    return total


def add_rows(dst, src):
    if len(dst.shape) == 3:
        for i in range(dst.shape[0]):
            dst[i] = plus(dst[i], src[i]).astype(BF)
        return

    def body(i, _):
        l, k = lax.div(i, RING), lax.rem(i, RING)
        dst[l, k] = plus(dst[l, k], src[l, k]).astype(BF)
        return 0

    lax.fori_loop(0, dst.shape[0] * RING, body, 0)


def weight_reduce(links, at, grads, total, bufs1, bufs2, outs):
    x, z, c = at.x, at.z, at.c
    ring_x, ring_z, mate = at.ring("x"), at.ring("z"), at.partner()
    arrays = grads.shape[0]
    swaps = [
        links.push(grads.at[:, k, :, 1 - c], total.at[:, k], mate) for k in range(RING)
    ]
    yield
    for k in range(RING):
        swaps[k].wait_recv()

        def body(i, _, k=k):
            l, j = lax.div(i, RING), lax.rem(i, RING)
            total[l, k, j] = plus(grads[l, k, j, c], total[l, k, j]).astype(BF)
            return 0

        lax.fori_loop(0, arrays * RING, body, 0)

    bufs = lambda ref, color: [ref.at[color, i] for i in range(6)]
    part_a = lambda k, h: total.at[:, :, k, rows_of(h)]
    part_b = lambda k, h: total.at[:, k, :, rows_of(2 + h)]
    a1 = ring_reduce(links, ring_x, part_a, bufs(bufs1, 0), add_rows)
    b1 = ring_reduce(links, ring_z, part_b, bufs(bufs1, 1), add_rows)
    for i in range(3):
        next(a1, None)
        next(b1, None)
        if i < 2:
            yield

    def close1(buf, own, h):
        one, two = (buf[3], buf[4]) if h == 0 else (buf[2], buf[5])

        def body(i, _):
            l, k = lax.div(i, RING), lax.rem(i, RING)
            own[l, k] = plus(own[l, k], one[l, k], two[l, k]).astype(BF)
            return 0

        lax.fori_loop(0, arrays * RING, body, 0)

    for h in range(2):
        close1(bufs(bufs1, 0), part_a(x, h), h)
        close1(bufs(bufs1, 1), part_b(z, h), h)
    part_a2 = lambda k, h: total.at[:, k, x, rows_of(h)]
    part_b2 = lambda k, h: total.at[:, z, k, rows_of(2 + h)]
    a2 = ring_reduce(links, ring_z, part_a2, bufs(bufs2, 0), add_rows)
    b2 = ring_reduce(links, ring_x, part_b2, bufs(bufs2, 1), add_rows)
    for i in range(3):
        next(a2, None)
        next(b2, None)
        if i < 2:
            yield
    for color, own in ((0, lambda h: part_a2(z, h)), (1, lambda h: part_b2(x, h))):
        buf = bufs(bufs2, color)
        for h in range(2):
            one, two = (buf[3], buf[4]) if h == 0 else (buf[2], buf[5])
            for l in range(arrays):
                outs[l][rows_of(2 * color + h)] = plus(own(h)[l], one[l], two[l])


def add_tokens(dst, src):
    for i in range(8):
        r = rows_of(i)
        dst[r] = plus(dst[r], src[r]).astype(BF)


def lanes_of(h):
    return pl.ds(512 * h, 512)


class TokenSum:
    def __init__(self, links, ring, part, land):
        self.part, self.land, self.p = part, [land.at[i] for i in range(6)], ring[0]
        self.steps = ring_reduce(
            links, ring, lambda k, h: part.at[k, :, lanes_of(h)], self.land, add_tokens, True
        )

    def produce(self, chunk):
        for h in range(2):

            def body(j, _, h=h):
                n = 2 * h + j
                value = chunk(n).astype(BF).reshape(RING, 128, 256)
                self.part[:, :, pl.ds(pl.multiple_of(n * 256, 256), 256)] = value
                return 0

            lax.fori_loop(0, 2, body, 0)
            next(self.steps)

    def rows(self, i):
        r, land = rows_of(i), self.land
        lo = plus(self.part[self.p, r, lanes_of(0)], land[3][r], land[4][r])
        hi = plus(self.part[self.p, r, lanes_of(1)], land[2][r], land[5][r])
        return jnp.concatenate([lo, hi], 1)


def quarter(n):
    return lax.div(n, 2), pl.ds(2 * lax.rem(n, 2), 2)


def inverse_rms(v):
    return lax.rsqrt(jnp.mean(v * v, -1, keepdims=True) + EPS)


def block_kernel(
    x_ref, gain1, wb, wc, wx, wo, taps_ref, gain2, cot_ref, wg, wu, wd,
    out_ref, gin_ref, n1_out, gb_out, gc_out, gx_out, conv_out, go_out, n2_out,
    gg_out, gu_out, gd_out,
    mix, ffn, h1, h2, cots, dmids, taps, bp, xp, cp, gext, conv, dext, ymix, dmix,
    mid, dmid, act, dgate, dup, part_mid, part_back, part_down, part_in, land,
    mix_g, mix_t, mix_b1, mix_b2, ffn_g, ffn_t, ffn_b1, ffn_b2, small, send, recv, local,
):
    at = Place()
    links = Links(send, recv, local)
    ring_y, ring_x, ring_z = at.ring("y"), at.ring("x"), at.ring("z")
    dp, t = lax.axis_index("dp"), lax.axis_index("tensor")
    n_dp = lax.axis_size("dp")
    p, zhi = at.y, at.zhi
    flip = t + 1 - 2 * zhi
    beside = (lax.rem(dp + n_dp + 2 * zhi - 1, n_dp), flip)
    own0 = [links.near(w, mix.at[i, at.z, at.x, at.c]) for i, w in enumerate((wb, wc, wx, wo))]
    own1 = [links.near(w, ffn.at[i, at.z, at.x, at.c]) for i, w in enumerate((wg, wu, wd))]
    for i in range(8):
        r = rows_of(i)
        v = x_ref[r]
        h1[p, r] = (v * inverse_rms(v) * gain1[...]).astype(BF)
    taps[zhi] = taps_ref[...]
    greet([*ring_y[1:4], *ring_x[1:4], *ring_z[1:4], at.partner(), beside])

    rows_half = lambda ref: lambda k, h: ref.at[k, pl.ds(64 * h, 64)]
    tok1 = ring_gather(links, ring_y, rows_half(h1))
    next(tok1)
    for copy in own0:
        copy.wait()
    mix_in = weight_gather(links, at, mix)
    next(mix_in)
    tap = links.push(taps_ref, taps.at[zhi], ring_z[3])
    for copy in own1:
        copy.wait()
    for i in range(8):
        r = rows_of(i)
        cots[p, r] = cot_ref[r].astype(BF)
    next(mix_in)
    next(tok1)
    next(mix_in)
    ffn_in = weight_gather(links, at, ffn)
    next(ffn_in)
    next(mix_in)
    next(mix_in)
    next(ffn_in)
    drain(tok1)
    drain(mix_in)

    def mixer(i):
        return jnp.concatenate(
            [mix[i, pl.ds(2 * s, 2)].reshape(1024, 128) for s in range(2)], 1
        )

    def mixer_rows(i, n):
        zz, xx = quarter(n)
        return jnp.concatenate(
            [mix[i, 2 * s + zz, xx].reshape(256, 128) for s in range(2)], 1
        )

    def ffn_half(i, s):
        return ffn[i, pl.ds(2 * s, 2)].reshape(1024, 576)

    def ffn_rows(i, s, n):
        zz, xx = quarter(n)
        return ffn[i, 2 * s + zz, xx].reshape(256, 576)

    def project(m, _):
        two = pl.ds(2 * m, 2)
        h = h1[two].reshape(256, 1024)
        b, x = dot(h, mixer(0)), dot(h, mixer(2))
        bp[two] = b.reshape(2, 128, 256)
        xp[two] = x.reshape(2, 128, 256)
        gext[two, pl.ds(8, 128)] = (b * x).reshape(2, 128, 256)
        return 0

    lax.fori_loop(0, 2, project, 0)
    tails = []
    for k in range(RING):
        to_dp = dp if k < 3 else lax.rem(dp + zhi, n_dp)
        tails.append(
            links.push(
                gext.at[k, pl.ds(128, 8)], gext.at[lax.rem(k + zhi, RING), pl.ds(0, 8)],
                (to_dp, flip),
            )
        )
    next(ffn_in)

    def project_c(m, _):
        two = pl.ds(2 * m, 2)
        cp[two] = dot(h1[two].reshape(256, 1024), mixer(1)).reshape(2, 128, 256)
        return 0

    lax.fori_loop(0, 2, project_c, 0)
    tap.wait_recv()
    for copy in tails:
        copy.wait_recv()
    row = lax.broadcasted_iota(jnp.int32, (128, 256), 0)
    tap_rows = jnp.concatenate([taps[0], taps[1]], 1)
    t0, t1, t2 = tap_rows[0:1], tap_rows[1:2], tap_rows[2:3]

    def keeps(r):
        begins = (r == 0) | (lax.rem(r * 128 + SEQ - OFFSET, SEQ) == 0)
        return jnp.where(begins | (r == n_dp * 8), 0.0, 1.0)

    def shifted(k):
        keep = keeps(dp * 8 + 2 * k + zhi)
        two, one = gext[k, pl.ds(6, 128)], gext[k, pl.ds(7, 128)]
        return jnp.where(row < 2, two * keep, two), jnp.where(row < 1, one * keep, one)

    def mixing(k, _):
        two, one = shifted(k)
        v = t0 * two + t1 * one + t2 * gext[k, pl.ds(8, 128)]
        conv[k] = v
        ymix[k] = (cp[k] * v).astype(BF)
        return 0

    lax.fori_loop(0, RING, mixing, 0)
    sum_mid = TokenSum(links, ring_y, part_mid, land.at[0])
    sum_mid.produce(lambda n: ndot(ymix[...].reshape(512, 256), mixer_rows(3, n)))
    next(ffn_in)
    next(sum_mid.steps)
    drain(sum_mid.steps)
    tok2 = ring_gather(links, ring_y, rows_half(h2), staged=True)
    for i in range(8):
        r = rows_of(i)
        v = x_ref[r] + sum_mid.rows(i)
        mid[r] = v
        h2[p, r] = (v * inverse_rms(v) * gain2[...]).astype(BF)
        if i % 4 == 3:
            next(tok2)
    tok_c = ring_gather(links, ring_y, rows_half(cots))
    next(tok_c)
    next(tok2)
    next(ffn_in)
    next(tok_c)
    drain(tok2)
    drain(tok_c)
    drain(ffn_in)

    def feed(i, _):
        s, m = lax.div(i, 2), lax.rem(i, 2)
        two = pl.ds(2 * m, 2)
        h = h2[two].reshape(256, 1024)
        gate, up = dot(h, ffn_half(0, s)), dot(h, ffn_half(1, s))
        dact = dot(cots[two].reshape(256, 1024), ffn_half(2, s))
        sig = jax.nn.sigmoid(gate)
        silu = gate * sig
        r = pl.ds(pl.multiple_of(m * 256, 256), 256)
        act[s, r] = (silu * up).astype(BF)
        dgate[s, r] = (dact * up * sig * (1.0 + gate * (1.0 - sig))).astype(BF)
        dup[s, r] = (dact * silu).astype(BF)
        return 0

    lax.fori_loop(0, 4, feed, 0)
    sum_back = TokenSum(links, ring_y, part_back, land.at[1])

    def back_chunk(n):
        v = ndot(dgate[0], ffn_rows(0, 0, n)) + ndot(dup[0], ffn_rows(1, 0, n))
        return v + ndot(dgate[1], ffn_rows(0, 1, n)) + ndot(dup[1], ffn_rows(1, 1, n))

    sum_back.produce(back_chunk)

    def ffn_grads(s, pairs):
        def body(n, _):
            zz, xx = quarter(n)
            cols = pl.ds(pl.multiple_of(n * 256, 256), 256)
            for i, tokens, right in pairs:
                left = tokens[:, :, cols].reshape(512, 256)
                g = tdot(left, right[s]).astype(BF)
                ffn_g[i, 2 * s + zz, xx] = g.reshape(2, 2, 64, 576)
            return 0

        lax.fori_loop(0, 4, body, 0)

    ffn_grads(0, ((0, h2, dgate), (1, h2, dup)))
    next(sum_back.steps)
    ffn_grads(1, ((0, h2, dgate), (1, h2, dup)))
    drain(sum_back.steps)
    tok3 = ring_gather(links, ring_y, rows_half(dmids), staged=True)
    norm2 = jnp.zeros((8, 1024), F32)
    for i in range(8):
        r = rows_of(i)
        dh = sum_back.rows(i)
        v = mid[r]
        r2 = inverse_rms(v)
        n2 = v * r2
        w = dh * n2
        norm2 = norm2 + w[:8] + w[8:]
        dn = dh * gain2[...]
        dm = cot_ref[r] + r2 * (dn - n2 * jnp.mean(dn * n2, -1, keepdims=True))
        dmid[r] = dm
        dmids[p, r] = dm.astype(BF)
        if i % 4 == 3:
            next(tok3)
    ffn_grads(0, ((2, cots, act),))
    next(tok3)
    ffn_grads(1, ((2, cots, act),))
    ffn_out = weight_reduce(links, at, ffn_g, ffn_t, ffn_b1, ffn_b2, (gg_out, gu_out, gd_out))
    next(ffn_out)
    sum_down = TokenSum(links, ring_y, part_down, land.at[2])
    sum_down.produce(
        lambda n: ndot(act[0], ffn_rows(2, 0, n)) + ndot(act[1], ffn_rows(2, 1, n))
    )
    drain(tok3)
    next(ffn_out)

    def spread(m, _):
        two = pl.ds(2 * m, 2)
        dy = dot(dmids[two].reshape(256, 1024), mixer(3)).reshape(2, 128, 256)
        dext[two, pl.ds(0, 128)] = dy * cp[two]
        dc = (dy * conv[two]).astype(BF).reshape(256, 256)
        dmix[pl.ds(pl.multiple_of(m * 256, 256), 256), pl.ds(256, 256)] = dc
        return 0

    lax.fori_loop(0, 2, spread, 0)
    heads = []
    for k in range(RING):
        to_dp = dp if k > 0 else lax.rem(dp + n_dp + zhi - 1, n_dp)
        heads.append(
            links.push(
                dext.at[k, pl.ds(0, 8)], dext.at[lax.rem(k + 3 + zhi, RING), pl.ds(128, 8)],
                (to_dp, flip),
            )
        )
    next(sum_down.steps)

    def mix_grads(i, tokens, right):
        def body(n, _):
            zz, xx = quarter(n)
            cols = pl.ds(pl.multiple_of(n * 256, 256), 256)
            g = tdot(tokens[:, :, cols].reshape(512, 256), right()).astype(BF)
            for s in range(2):
                mix_g[i, 2 * s + zz, xx] = g[:, 128 * s : 128 * s + 128].reshape(2, 2, 64, 128)
            return 0

        lax.fori_loop(0, 4, body, 0)

    mix_grads(3, dmids, lambda: ymix[...].reshape(512, 256))
    for copy in heads:
        copy.wait_recv()

    def unmix(k, carry):
        keep = keeps(dp * 8 + 2 * k + zhi + 1)
        d = dext[k, pl.ds(0, 128)]
        one, two = dext[k, pl.ds(1, 128)], dext[k, pl.ds(2, 128)]
        one = jnp.where(row >= 127, one * keep, one)
        two = jnp.where(row >= 126, two * keep, two)
        dg = t2 * d + t1 * one + t0 * two
        r = pl.ds(pl.multiple_of(k * 128, 128), 128)
        dmix[r, pl.ds(0, 256)] = (dg * xp[k]).astype(BF)
        dmix[r, pl.ds(512, 256)] = (dg * bp[k]).astype(BF)
        g2, g1 = shifted(k)
        terms = (g2, g1, gext[k, pl.ds(8, 128)])
        return tuple(c + jnp.sum(d * v, 0, keepdims=True) for c, v in zip(carry, terms))

    zero = jnp.zeros((1, 256), F32)
    conv_sums = lax.fori_loop(0, RING, unmix, (zero, zero, zero))
    sum_in = TokenSum(links, ring_y, part_in, land.at[3])

    def in_chunk(n):
        w = jnp.concatenate([mixer_rows(i, n) for i in range(3)], 1)
        return ndot(dmix[...], w)

    sum_in.produce(in_chunk)
    next(ffn_out)
    drain(sum_down.steps)
    for i in range(8):
        r = rows_of(i)
        out_ref[r] = mid[r] + sum_down.rows(i)
    for i in range(3):
        mix_grads(i, h1, lambda i=i: dmix[:, 256 * i : 256 * i + 256])
        if i == 1:
            next(sum_in.steps)
    mix_out = weight_reduce(links, at, mix_g, mix_t, mix_b1, mix_b2, (gb_out, gc_out, gx_out, go_out))
    next(mix_out)
    next(ffn_out)
    next(mix_out)
    drain(sum_in.steps)
    norm1 = jnp.zeros((8, 1024), F32)
    for i in range(8):
        r = rows_of(i)
        dh = sum_in.rows(i)
        v = x_ref[r]
        r1 = inverse_rms(v)
        n1 = v * r1
        w = dh * n1
        norm1 = norm1 + w[:8] + w[8:]
        dn = dh * gain1[...]
        gin_ref[r] = dmid[r] + r1 * (dn - n1 * jnp.mean(dn * n1, -1, keepdims=True))
    small[0, p] = jnp.zeros((8, 1024), F32)
    small[0, p, 0:1] = jnp.sum(norm1, 0, keepdims=True)
    small[0, p, 1:2] = jnp.sum(norm2, 0, keepdims=True)
    for i in range(3):
        small[0, p, pl.ds(2 + i, 1), pl.ds(pl.multiple_of(p * 256, 256), 256)] = conv_sums[i]
    for s, ring in enumerate((ring_y, ring_x, ring_z)):
        pos = ring[0]
        copies = [links.push(small.at[s, pos], small.at[s, pos], dev) for dev in ring[1:4]]
        next(ffn_out, None)
        next(mix_out, None)
        for copy in copies:
            copy.wait_recv()
        value = (small[s, 0] + small[s, 1]) + (small[s, 2] + small[s, 3])
        if s < 2:
            small[s + 1, (ring_x, ring_z)[s][0]] = value
        else:
            small[3, at.c] = value
    copy = links.push(small.at[3, at.c], small.at[3, at.c], at.partner())
    next(mix_out, None)
    copy.wait_recv()
    value = small[3, 0] + small[3, 1]
    n1_out[...] = value[0:1]
    n2_out[...] = value[1:2]
    small[3, 2] = value
    conv_out[...] = small[3, 2, pl.ds(2, 3), pl.ds(pl.multiple_of(t * 128, 128), 128)]
    drain(ffn_out)
    drain(mix_out)
    links.close()


VM = pl.BlockSpec(memory_space=pltpu.VMEM)
ANY = pl.BlockSpec(memory_space=pl.ANY)


def per_device(
    block_in, norm1_gain, w_b, w_c, w_x, conv_w, w_out, norm2_gain, w_gate, w_up, w_down, out_cot
):
    f = lambda *shape: jax.ShapeDtypeStruct(shape, F32)
    bf = lambda *shape: pltpu.VMEM(shape, BF)
    fl = lambda *shape: pltpu.VMEM(shape, F32)
    tokens = bf(RING, 128, 1024)
    plane = fl(RING, 128, 256)
    sems = pltpu.SemaphoreType.DMA
    outs = pl.pallas_call(
        block_kernel,
        out_shape=[
            f(128, 1024), f(128, 1024), f(1, 1024), f(64, 128), f(64, 128), f(64, 128),
            f(3, 128), f(64, 128), f(1, 1024), f(64, 576), f(64, 576), f(64, 576),
        ],
        in_specs=[VM, VM, ANY, ANY, ANY, ANY, VM, VM, VM, ANY, ANY, ANY],
        out_specs=[VM] * 12,
        scratch_shapes=[
            bf(4, 4, 4, 2, 64, 128), bf(3, 4, 4, 2, 64, 576),
            tokens, tokens, tokens, tokens,
            fl(2, 3, 128), plane, plane, plane, fl(RING, 136, 256), plane, fl(RING, 136, 256),
            bf(RING, 128, 256), bf(512, 768), fl(128, 1024), fl(128, 1024),
            bf(2, 512, 576), bf(2, 512, 576), bf(2, 512, 576),
            tokens, tokens, tokens, tokens, bf(4, 6, 128, 512),
            bf(4, 4, 4, 2, 64, 128), bf(4, 4, 4, 64, 128), bf(2, 6, 4, 4, 16, 128),
            bf(2, 6, 4, 16, 128),
            bf(3, 4, 4, 2, 64, 576), bf(3, 4, 4, 64, 576), bf(2, 6, 3, 4, 16, 576),
            bf(2, 6, 3, 16, 576),
            fl(4, RING, 8, 1024), sems((256,)), sems((256,)), sems((8,)),
        ],
        compiler_params=pltpu.CompilerParams(
            collective_id=0, has_side_effects=True, vmem_limit_bytes=VMEM_LIMIT
        ),
    )(
        block_in, norm1_gain[None, :], w_b, w_c, w_x, w_out.T, conv_w, norm2_gain[None, :],
        out_cot, w_gate, w_up, w_down.T,
    )
    out, gin, n1, gb, gc, gx, gconv, go, n2, gg, gu, gd = outs
    return (out, gin, n1[0], gb, gc, gx, gconv, go.T, n2[0], gg, gu, gd.T)


def solution(mesh):
    tok, mat, tam = P(("dp", "tensor"), None), P("dp", "tensor"), P("tensor", "dp")
    taps = P(None, "tensor")
    return jax.shard_map(
        per_device,
        mesh=mesh,
        in_specs=(tok, P(), mat, mat, mat, taps, tam, P(), mat, mat, tam, tok),
        out_specs=(tok, tok, P(), mat, mat, mat, taps, tam, P(), mat, mat, tam),
        check_vma=False,
    )
```

time: 1060 us -> 156 us (0.15)
  waiting for transfers between devices: 795 us -> 0 us
  Pallas kernels: 0 us -> 145 us
  blocking collectives: 141 us -> 0 us
  matrix products: 66.4 us -> 0 us
  other arithmetic: 26.6 us -> 0 us
  between operations: 16.1 us -> 0.69 us
    reduce_scatter x11 -> x0, waiting for transfers between devices: 585 us -> none  [the longest x4 243 us: seq_scatter(): lax.psum_scatter(values.astype(jnp.bfloat16), 'tensor', scatter_dimension...]
    all_gather x7 -> x0, waiting for transfers between devices: 207 us -> none  [the longest x4 149 us: seq_gather(): lax.all_gather(values.astype(jnp.bfloat16), 'tensor', axis=0, tiled=True)]
    pallas_call x0 -> x1, Pallas kernels: none -> 145 us  [per_device(): pl.pallas_call(block_kernel, out_shape=[f(128, 1024), f(128, 1024), f(1,...]
    all_gather x4 -> x0, blocking collectives: 75 us -> none  [the longest x1 21.1 us: per_device(): lax.all_gather(w_b, 'dp', axis=0, tiled=True)]
    dot_general x21 -> x0, matrix products: 66.4 us -> none  [the longest x7 22.4 us: tdot(): lax.dot_general(left, right, (((0,), (0,)), ((), ())), preferred_element_...]
    psum x1 -> x0, blocking collectives: 66 us -> none  [per_device(): lax.psum((part_n1, part_n2, placed), ('dp', 'tensor'))]
    convert_element_type x13 -> x0, other arithmetic: 18.8 us -> none  [the longest x4 6.26 us: seq_gather(): values.astype(jnp.bfloat16)]
  transfers between devices with their start and end apart: 20 -> 0, of which waited for: 16 -> 0; matrix products, arithmetic and copies ran while one was open for 7% -> 0% of each run, Pallas kernels for 0% -> 0%
where the time goes in v2:
time: 156 us; the launch traced here: 155 us
  Pallas kernels  145 us (93%)
  local copies, waits for them, and re-layouts  9.73 us (6%)
    pallas_call x1, Pallas kernels, per_device(): pl.pallas_call(block_kernel, out_shape=[f(128, 1024), f(128, 1024), f(1,...  145 us
    unnamed x34, local copies, waits for them, and re-layouts  9.73 us

profile of v2, /device:TPU:0, one launch (start us, length us, event | category | flops | bytes accessed | tf_op | source)
XLA Modules:
  0.0 155.2 jit_solution(445053616275428137)
XLA Ops:
  0.6 144.8 %shard_map.211 = (f32[128,1024]{1,0:T(8,128)}, f32[128,1024]{1,0:T(8,128)}, f32[1,1024]{1,0:T(1,128)}, f32[64,128]{1,0:T(8,128)}, f32[64,128]{1,0:T(8,128)}, /*i...) custom-call(f32[128,1024]{1,0:T(8,128)} %x_ref.1, ...), custom_call_target="tpu_custom_call" | custom-call | tf_op jit(solution)/shard_map/pallas_call | solution.py:649
  145.5 0.0 copy-start
  145.5 1.9 %copy.36 = f32[128,1024]{1,0:T(8,128)} copy(f32[128,1024]{1,0:T(8,128)} %get-tuple-element.48) | data formatting | bytes 1048576
  147.4 0.0 copy-done
  147.4 0.0 copy-start.9
  147.4 0.0 copy-start.7
  147.4 0.0 copy-start.6
  147.4 0.0 copy-start.5
  147.5 0.8 copy.37
  148.3 0.0 copy-done.9
  148.3 0.0 copy-start.3
  148.3 0.6 copy.38
  148.9 0.0 copy-done.7
  148.9 0.6 copy.39
  149.5 0.0 copy-done.6
  149.5 0.6 copy.40
  150.1 0.0 copy-done.5
  150.1 0.0 copy-start.10
  150.1 0.0 copy-start.4
  150.1 0.6 copy.41
  150.7 0.1 copy-done.10
  150.8 0.6 copy.42
  151.4 0.0 copy-done.4
  151.4 0.0 copy-start.8
  151.4 0.6 copy.43
  152.0 0.1 copy-done.8
  152.0 0.6 copy.44
  152.6 0.0 copy-done.3
  152.6 0.0 copy-start.2
  152.6 0.7 copy.45
  153.3 0.3 copy-done.2
  153.6 0.0 copy-start.1
  153.6 0.7 copy.46
  154.3 0.3 copy-done.1
  154.6 0.7 copy.47
Async XLA Ops:
  145.5 2.0 %copy-start = (f32[128,1024]{1,0:T(8,128)S(1)}, f32[128,1024]{1,0:T(8,128)}, u32[]{:S(2)}) copy-start(f32[128,1024]{1,0:T(8,128)} %get-tuple-element.49) | copy-start | bytes 1572868
  147.4 0.8 copy-start.9
  147.4 1.4 copy-start.7
  147.4 2.0 %copy-start.6 = (f32[64,128]{1,0:T(8,128)S(1)}, f32[64,128]{1,0:T(8,128)}, u32[]{:S(2)}) copy-start(f32[64,128]{1,0:T(8,128)} %get-tuple-element.52) | copy-start | bytes 98308
  147.4 2.6 %copy-start.5 = (f32[64,128]{1,0:T(8,128)S(1)}, f32[64,128]{1,0:T(8,128)}, u32[]{:S(2)}) copy-start(f32[64,128]{1,0:T(8,128)} %get-tuple-element.53) | copy-start | bytes 98308
  148.3 4.4 %copy-start.3 = (f32[64,576]{1,0:T(8,128)S(1)}, f32[64,576]{1,0:T(8,128)}, u32[]{:S(2)}) copy-start(f32[64,576]{1,0:T(8,128)} %get-tuple-element.57) | copy-start | bytes 442372
  150.1 0.7 copy-start.10
  150.1 1.3 copy-start.4
  151.4 0.7 copy-start.8
  152.6 1.0 copy-start.2
  153.6 1.0 copy-start.1
